TPU v7x, 256 devices: a whole 4x4x8 slice. The times are simulated.
256 devices in a mesh: space: 64 (over z, x, core), member: 4 (over y).
Axes of the slice: x: 4, y: 4, z: 8, core: 2. Of those that a mesh axis runs over, the one named last changes fastest.
Arguments:
- head_start: float32 [32, 4, 2048, 256], P('member', None, 'space'), parts along dimension 0, may hold values from -4 to 4
- recharge: float32 [32, 2048, 256], P('member', 'space'), parts along dimension 0, may hold values from -3 to 3
- section_start: float32 [32, 65536], P('member', 'space'), parts along dimension 0, may hold values from -4 to 4
- inflow: float32 [32, 65536], P('member', 'space'), parts along dimension 0, may hold values from -4 to 4
- soil_class: int32 [4, 2048, 256], P(None, 'space'), may hold values from 0 to 11
- class_conduct: float32 [12], replicated, may hold values from 0.5 to 4
- class_alpha: float32 [12], replicated, may hold values from 0.3 to 2
- capacity: float32 [4, 2048, 256], P(None, 'space'), may hold values from 0.5 to 2
- river_cell: int32 [64, 6, 512], P('space'), may hold values from -1 to 8191, as said below
- river_reach: int32 [64, 6, 512], P('space'), may hold values from -1 to 1023, as said below
- river_cond: float32 [64, 6, 512], P('space'), may hold values from 0.5 to 2
- reach_rate: float32 [65536], P('space'), may hold values from 0.2 to 1
Outputs:
- water_head: float32 [32, 4, 2048, 256], P('member', None, 'space'), parts along dimension 0
- reach_section: float32 [32, 65536], P('member', 'space'), parts along dimension 0
There are 4 independent parts, one for each index of `member`. A program takes and returns all parts, laid end to end along the dimension named above; an argument that names none is the same for every part. Nothing has to cross between parts.
Inputs may be any that keep to these rules, and one draw needn't show every extreme that they name: `river_reach`: -1 marks an empty slot. Otherwise slot j of bucket b of tile t names a reach of that bucket's owner, which lies on the grid. The live slots of a bucket come first. Every tile has a bucket with all 512 slots live, and in every draw all buckets aimed at some one tile are full. `river_cell`: -1 exactly where river_reach is -1; otherwise a top-layer column x * 256 + y with x counted within the tile. A column may carry several slots.
All inputs are finite; a program needn't handle non-finite values.
Results may differ from a plain program's by a relative error of at most 0.00002.
Values sent between devices are 32-bit elements; how exact they have to be, the bound alone decides.
A program may use at most 64 MiB of HBM per device.

v0:
```python
import jax
import jax.numpy as jnp
from jax import lax
from jax.sharding import PartitionSpec as P

PICARD = 2
SWEEPS = 3


vertical_ratio = 0.5


def padded_2(block, sides, width):
    for axis, dim in sides:
        count = lax.axis_size(axis)
        forward = [(i, i + 1) for i in range(count - 1)]
        backward = [(target, source) for source, target in forward]
        low = lax.ppermute(
            lax.slice_in_dim(block, block.shape[dim] - width, None, axis=dim), axis, forward
        )
        high = lax.ppermute(lax.slice_in_dim(block, 0, width, axis=dim), axis, backward)
        block = jnp.concatenate([low, block, high], axis=dim)
    return block


def harmonic(first, second):
    return 2.0 * first * second / (first + second)


def place_out(buckets, position, tile_count, reach_span):
    near_count = 2 * reach_span + 1
    lead_size, bucket_count, slot_count = buckets.shape
    holder = jnp.zeros((lead_size, tile_count + 2 * reach_span, slot_count), buckets.dtype)
    holder = lax.dynamic_update_slice_in_dim(holder, buckets[:, :near_count], position, 1)
    holder = holder[:, reach_span : reach_span + tile_count]
    far_index = (position + tile_count // 2) % tile_count
    return lax.dynamic_update_slice_in_dim(holder, buckets[:, near_count:], far_index, 1)


def pick_in(received, position, tile_count, reach_span, flipped):
    near_count = 2 * reach_span + 1
    padded = jnp.pad(received, ((0, 0), (reach_span, reach_span), (0, 0)))
    near_part = lax.dynamic_slice_in_dim(padded, position, near_count, 1)
    if flipped:
        near_part = jnp.flip(near_part, 1)
    far_index = (position + tile_count // 2) % tile_count
    far_part = lax.dynamic_slice_in_dim(received, far_index, 1, 1)
    return jnp.concatenate([near_part, far_part], 1)


def reorder_near(buckets, reach_span):
    near_count = 2 * reach_span + 1
    return jnp.concatenate([jnp.flip(buckets[:, :near_count], 1), buckets[:, near_count:]], 1)


def forward_request(request, position, tile_count, reach_span):
    outgoing = place_out(request, position, tile_count, reach_span)
    received = lax.all_to_all(outgoing, "space", split_axis=1, concat_axis=1, tiled=True)
    arrived = pick_in(received, position, tile_count, reach_span, True)
    return arrived


def forward_leakage(leakage, position, tile_count, reach_span):
    outgoing = place_out(leakage, position, tile_count, reach_span)
    received = lax.all_to_all(outgoing, "space", split_axis=1, concat_axis=1, tiled=True)
    arrived = pick_in(received, position, tile_count, reach_span, True)
    return arrived


def backward_section(reply, position, tile_count, reach_span):
    outgoing = place_out(reorder_near(reply, reach_span), position, tile_count, reach_span)
    received = lax.all_to_all(outgoing, "space", split_axis=1, concat_axis=1, tiled=True)
    returned = pick_in(received, position, tile_count, reach_span, False)
    return returned


def extend(head_now):
    return padded_2(head_now, (("space", 2),), 1)


def faces(conduct, conduct_pad):
    along_y = jnp.pad(conduct, ((0, 0), (0, 0), (0, 0), (1, 1)))
    along_z = jnp.pad(conduct, ((0, 0), (1, 1), (0, 0), (0, 0)))
    return (
        harmonic(conduct, conduct_pad[:, :, 2:]),
        harmonic(conduct, conduct_pad[:, :, :-2]),
        harmonic(conduct, along_y[..., 2:]),
        harmonic(conduct, along_y[..., :-2]),
        vertical_ratio * harmonic(conduct, along_z[:, 2:]),
        vertical_ratio * harmonic(conduct, along_z[:, :-2]),
    )


def relax(head_now, head_pad, source_term, diagonal, links):
    along_y = jnp.pad(head_now, ((0, 0), (0, 0), (0, 0), (1, 1)))
    along_z = jnp.pad(head_now, ((0, 0), (1, 1), (0, 0), (0, 0)))
    total = source_term + links[0] * head_pad[:, :, 2:] + links[1] * head_pad[:, :, :-2]
    total = total + links[2] * along_y[..., 2:] + links[3] * along_y[..., :-2]
    total = total + links[4] * along_z[:, 2:] + links[5] * along_z[:, :-2]
    return total / diagonal


def body(
    head_start,
    recharge,
    section_start,
    inflow,
    soil_class,
    class_conduct,
    class_alpha,
    capacity,
    river_cell,
    river_reach,
    river_cond,
    reach_rate,
):
    members, layers, row_count, col_count = head_start.shape
    tile_count = lax.axis_size("space")
    position = lax.axis_index("space")
    bucket_count = river_reach.shape[1]
    reach_span = (bucket_count - 2) // 2
    reach_count = section_start.shape[1]
    class_ids = jnp.arange(class_conduct.shape[0], dtype=jnp.int32)[:, None, None, None]
    matches = soil_class[None] == class_ids
    cell_conduct = jnp.sum(jnp.where(matches, class_conduct[:, None, None, None], 0.0), 0)
    cell_alpha = jnp.sum(jnp.where(matches, class_alpha[:, None, None, None], 0.0), 0)
    live_slot = river_reach[0] >= 0
    columns = jnp.where(live_slot, river_cell[0], 0).reshape(-1)
    weight = jnp.where(live_slot, river_cond[0], 0.0)
    col_cond = jnp.zeros((row_count * col_count,), jnp.float32).at[columns].add(weight.reshape(-1))
    col_cond = col_cond.reshape(row_count, col_count)
    arrived = forward_request(river_reach + 1, position, tile_count, reach_span)
    owner_live = arrived[0] > 0
    owner_ids = jnp.maximum(arrived[0] - 1, 0).reshape(-1)
    section_now = section_start
    head_now = head_start
    for outer in range(PICARD):
        reply = section_now[:, owner_ids].reshape(members, bucket_count, -1)
        fetched = backward_section(reply, position, tile_count, reach_span)
        river_rhs = jnp.zeros((members, row_count * col_count), jnp.float32)
        river_rhs = river_rhs.at[:, columns].add((weight[None] * fetched).reshape(members, -1))
        river_rhs = river_rhs.reshape(members, row_count, col_count)
        head_pad = extend(head_now)
        conduct = cell_conduct * jnp.exp(cell_alpha * jnp.minimum(head_now, 0.0))
        conduct_pad = padded_2(conduct, (("space", 2),), 1)
        links = faces(conduct, conduct_pad)
        diagonal = capacity + links[0] + links[1] + links[2] + links[3] + links[4] + links[5]
        diagonal = diagonal.at[:, 0].add(col_cond)
        source_term = capacity * head_start
        source_term = source_term.at[:, 0].add(recharge + river_rhs)
        for sweep in range(SWEEPS):
            if sweep > 0:
                head_pad = extend(head_now)
            head_now = relax(head_now, head_pad, source_term, diagonal, links)
        top_head = (
            head_now[:, 0].reshape(members, -1)[:, columns].reshape(members, bucket_count, -1)
        )
        leakage = weight[None] * (fetched - top_head)
        delivered = forward_leakage(leakage, position, tile_count, reach_span)
        leak_live = jnp.where(owner_live[None], delivered, 0.0).reshape(members, -1)
        reach_leak = jnp.zeros((members, reach_count), jnp.float32).at[:, owner_ids].add(leak_live)
        section_now = section_start + reach_rate[None] * (inflow - reach_leak)
    return (head_now, section_now)


def solution(mesh):
    return jax.shard_map(
        body,
        mesh=mesh,
        in_specs=(
            P("member", None, "space", None),
            P("member", "space", None),
            P("member", "space"),
            P("member", "space"),
            P(None, "space", None),
            P(),
            P(),
            P(None, "space", None),
            P("space", None, None),
            P("space", None, None),
            P("space", None, None),
            P("space"),
        ),
        out_specs=(P("member", None, "space", None), P("member", "space")),
        check_vma=False,
    )
```

profile of v0, /device:TPU:1, one launch (start us, length us, event | category | flops | bytes accessed | tf_op | source)
XLA Modules:
  0.0 412.7 jit_solution(17092031859194672880)
XLA Ops:
  3.4 13.0 %all-to-all-start = ((s32[1,64,512]{2,0,1:T(1,128)}), s32[1,64,512]{2,0,1:T(1,128)S(1)}, u32[]{:S(2)}, u32[]{:S(2)}) async-start(s32[1,64,512]{2,0,1:T(1,128)} %constant_dynamic-update-slice_fusion.2), calls=%async_computation | async-start | bytes 262144 | tf_op jit(solution)/shard_map/all_to_all | solution.py:58
  28.9 11.9 %gather_fusion = f32[3072,8]{1,0:T(8,128)} fusion(f32[8,1024]{0,1:T(8,128)} %copy.84, s32[3072]{0:T(1024)S(1)} %broadcast_clamp_fusion.1), kind=kCustom, calls=%fused_computation | custom fusion | bytes 208896 | tf_op jit(solution)/shard_map/gather | solution.py:138
  49.6 11.5 %all-to-all-start.1 = ((f32[8,64,512]{2,0,1:T(8,128)}), f32[8,64,512]{2,0,1:T(8,128)}, u32[]{:S(2)}, u32[]{:S(2)}) async-start(f32[8,64,512]{2,0,1:T(8,128)} %constant_dynamic-update-slice_fusion.1), calls=%async_computation.1 | async-start | bytes 2097152 | tf_op jit(solution)/shard_map/all_to_all | solution.py:72
  69.0 18.3 %scatter_custom_fusion.1 = f32[8192]{0:T(1024)S(1)} fusion(s32[3072]{0:T(1024)S(1)} %bitcast.65, f32[3072]{0:T(1024)S(1)} %bitcast.57, f32[]{:T(128)} %constant.138.clone.1), kind=kCustom, calls=%fused_computation.207 | custom fusion | flops 3072 | bytes 32772 | tf_op jit(solution)/shard_map/scatter-add | solution.py:130
  88.0 3.6 add_add_fusion.1
  97.2 21.1 %scatter_custom_fusion = f32[8,8192]{0,1:T(8,128)} fusion(s32[3072]{0:T(1024)} %bitcast.66, f32[3072,8]{1,0:T(8,128)} %copy.87, f32[]{:T(128)} %constant.138.clone.1), kind=kCustom, calls=%fused_computation.11 | custom fusion | flops 24576 | bytes 262656 | tf_op jit(solution)/shard_map/scatter-add | solution.py:141
  123.1 4.9 %fusion.9 = f32[8,4,32,256]{3,2,1,0:T(8,128)S(1)} fusion(f32[8,4,32,256]{3,2,1,0:T(8,128)S(1)} %fusion.95, f32[8,4,32,256]{3,2,1,0:T(8,128)S(1)} %copy-done.6, f32[8,4,32,256]{3,2,1,0:T(8,128)} %param.20, f32[8,4,32,256]{3,2,1,0:T(8,128)} %get-tuple-element.69, f32[8,4,32,256]{3,2,1,0:T(8,128)} %get-tuple-element.70, ...), kind=kLoop, calls=%fused_computation.57 | loop fusion | flops 6291456 | bytes 9568256 | tf_op jit(solution)/shard_map/div | solution.py:100
  139.5 4.4 %collective-permute-start.7 = (f32[8,4,1,256]{3,2,1,0:T(1,128)S(1)}, f32[8,4,1,256]{3,2,1,0:T(1,128)S(1)}, u32[]{:S(2)}, u32[]{:S(2)}) collective-permute-start(f32[8,4,1,256]{3,2,1,0:T(1,128)S(1)} %get-tuple-element.81), channel_id=1, source_target_pairs={{0,4},{4,8},{8,12},{12,16},{16,20},{20,24},{24,28},{28,32},{32,36}... | collective-permute-start | bytes 98312 | tf_op jit(solution)/shard_map/ppermute | solution.py:18
  152.1 10.3 %gather_fusion.1 = f32[3072,8]{1,0:T(8,128)S(1)} fusion(f32[8,8192]{0,1:T(8,128)} %bitcast.46, s32[3072]{0:T(1024)S(1)} %copy-done.32), kind=kCustom, calls=%fused_computation.1 | custom fusion | bytes 208896 | tf_op jit(solution)/shard_map/gather | solution.py:156
  164.7 18.8 %all-to-all-start.2 = ((f32[8,64,512]{2,0,1:T(8,128)}), f32[8,64,512]{2,0,1:T(8,128)S(1)}, u32[]{:S(2)}, u32[]{:S(2)}) async-start(f32[8,64,512]{2,0,1:T(8,128)} %slice_dynamic-update-slice_fusion.3), calls=%async_computation.2 | async-start | bytes 2097152 | tf_op jit(solution)/shard_map/all_to_all | solution.py:65
  183.6 28.1 %all-to-all-done.2 = f32[8,64,512]{2,0,1:T(8,128)S(1)} async-done(((f32[8,64,512]{2,0,1:T(8,128)}), f32[8,64,512]{2,0,1:T(8,128)S(1)}, u32[]{:S(2)}, u32[]{:S(2)}) %all-to-all-start.2) | async-done | bytes 1048608 | tf_op jit(solution)/shard_map/all_to_all | solution.py:65
  212.3 19.1 %scatter_custom_fusion.2 = f32[8,1024]{0,1:T(8,128)S(1)} fusion(s32[3072]{0:T(1024)} %bitcast.63, f32[3072,8]{1,0:T(8,128)S(1)} %copy.91, f32[]{:T(128)} %constant.138.clone.1), kind=kCustom, calls=%fused_computation.181 | custom fusion | flops 24576 | bytes 33280 | tf_op jit(solution)/shard_map/scatter-add | solution.py:161
  231.8 10.9 %gather_fusion.2 = f32[3072,8]{1,0:T(8,128)} fusion(f32[8,1024]{0,1:T(8,128)S(1)} %copy.93, s32[3072]{0:T(1024)S(1)} %copy-done.35), kind=kCustom, calls=%fused_computation.2 | custom fusion | bytes 208896 | tf_op jit(solution)/shard_map/gather | solution.py:138
  247.4 5.5 %all-to-all-start.3 = ((f32[8,64,512]{2,0,1:T(8,128)}), f32[8,64,512]{2,0,1:T(8,128)S(1)}, u32[]{:S(2)}, u32[]{:S(2)}) async-start(f32[8,64,512]{2,0,1:T(8,128)} %constant_dynamic-update-slice_fusion), calls=%async_computation.3 | async-start | bytes 2097152 | tf_op jit(solution)/shard_map/all_to_all | solution.py:72
  253.0 3.5 collective-permute-start.10
  260.2 3.6 collective-permute-start.11
  268.8 13.8 %all-to-all-done.3 = f32[8,64,512]{2,0,1:T(8,128)S(1)} async-done(((f32[8,64,512]{2,0,1:T(8,128)}), f32[8,64,512]{2,0,1:T(8,128)S(1)}, u32[]{:S(2)}, u32[]{:S(2)}) %all-to-all-start.3) | async-done | bytes 1048608 | tf_op jit(solution)/shard_map/all_to_all | solution.py:72
  284.4 21.1 %scatter_custom_fusion.3 = f32[8,8192]{0,1:T(8,128)} fusion(s32[3072]{0:T(1024)} %bitcast.67, f32[3072,8]{1,0:T(8,128)} %copy.96, f32[]{:T(128)} %constant.138.clone.1), kind=kCustom, calls=%fused_computation.9 | custom fusion | flops 24576 | bytes 262656 | tf_op jit(solution)/shard_map/scatter-add | solution.py:141
  309.7 5.3 %fusion.36 = f32[8,4,32,256]{3,2,1,0:T(8,128)S(1)} fusion(f32[8,4,32,256]{3,2,1,0:T(8,128)S(1)} %fusion.94, f32[8,4,32,256]{3,2,1,0:T(8,128)S(1)} %copy-done.2, f32[8,4,32,256]{3,2,1,0:T(8,128)} %copy-done.10, f32[8,4,32,256]{3,2,1,0:T(8,128)} %get-tuple-element.62, f32[8,4,32,256]{3,2,1,0:T(8,128)} %get-tuple-element.63, ...), kind=kLoop, calls=%fused_computation.84 | loop fusion | flops 6291456 | bytes 9568256 | tf_op jit(solution)/shard_map/div | solution.py:100
  317.1 3.5 collective-permute-start.13
  325.7 4.2 %collective-permute-start.15 = (f32[8,4,1,256]{3,2,1,0:T(1,128)S(1)}, f32[8,4,1,256]{3,2,1,0:T(1,128)S(1)}, u32[]{:S(2)}, u32[]{:S(2)}) collective-permute-start(f32[8,4,1,256]{3,2,1,0:T(1,128)S(1)} %get-tuple-element.73), channel_id=1, source_target_pairs={{0,4},{4,8},{8,12},{12,16},{16,20},{20,24},{24,28},{28,32},{32,36}... | collective-permute-start | bytes 98312 | tf_op jit(solution)/shard_map/ppermute | solution.py:18
  336.8 10.3 %gather_fusion.3 = f32[3072,8]{1,0:T(8,128)S(1)} fusion(f32[8,8192]{0,1:T(8,128)} %bitcast.45, s32[3072]{0:T(1024)S(1)} %copy-done.33), kind=kCustom, calls=%fused_computation.3 | custom fusion | bytes 208896 | tf_op jit(solution)/shard_map/gather | solution.py:156
  347.8 44.3 %all_to_all.25 = f32[8,64,512]{2,0,1:T(8,128)S(1)} all-to-all(f32[8,64,512]{2,0,1:T(8,128)S(1)} %slice_dynamic-update-slice_fusion.2), channel_id=1, replica_groups=mesh['space'=64,'member'=4] {'space'}, dimensions={1} | all-to-all | bytes 2097152 | tf_op jit(solution)/shard_map/all_to_all | solution.py:65
  392.7 19.1 %scatter_custom_fusion.4 = f32[8,1024]{0,1:T(8,128)S(1)} fusion(s32[3072]{0:T(1024)} %bitcast.64, f32[3072,8]{1,0:T(8,128)S(1)} %copy.100, f32[]{:T(128)} %constant.138.clone.1), kind=kCustom, calls=%fused_computation.179 | custom fusion | flops 24576 | bytes 33280 | tf_op jit(solution)/shard_map/scatter-add | solution.py:161
  (220 shorter events, 100.5 us)
Async XLA Ops:
  3.4 24.1 %all-to-all-start = ((s32[1,64,512]{2,0,1:T(1,128)}), s32[1,64,512]{2,0,1:T(1,128)S(1)}, u32[]{:S(2)}, u32[]{:S(2)}) async-start(s32[1,64,512]{2,0,1:T(1,128)} %constant_dynamic-update-slice_fusion.2), calls=%async_computation | async-start | bytes 262144 | tf_op jit(solution)/shard_map/all_to_all | solution.py:58
  19.6 68.4 %collective-permute-start = (f32[8,4,1,256]{3,2,1,0:T(1,128)}, f32[8,4,1,256]{3,2,1,0:T(1,128)}, u32[]{:S(2)}, u32[]{:S(2)}) collective-permute-start(f32[8,4,1,256]{3,2,1,0:T(1,128)} %get-tuple-element.89), channel_id=1, source_target_pairs={{4,0},{8,4},{12,8},{16,12},{20,16},{24,20},{28,24},{32,28},{36,32}... | collective-permute-start | bytes 98312 | tf_op jit(solution)/shard_map/ppermute | solution.py:21
  22.0 66.0 %collective-permute-start.2 = (f32[8,4,1,256]{3,2,1,0:T(1,128)}, f32[8,4,1,256]{3,2,1,0:T(1,128)}, u32[]{:S(2)}, u32[]{:S(2)}) collective-permute-start(f32[8,4,1,256]{3,2,1,0:T(1,128)} %get-tuple-element.88), channel_id=1, source_target_pairs={{0,4},{4,8},{8,12},{12,16},{16,20},{20,24},{24,28},{28,32},{32,36}... | collective-permute-start | bytes 98312 | tf_op jit(solution)/shard_map/ppermute | solution.py:18
  49.6 42.1 %all-to-all-start.1 = ((f32[8,64,512]{2,0,1:T(8,128)}), f32[8,64,512]{2,0,1:T(8,128)}, u32[]{:S(2)}, u32[]{:S(2)}) async-start(f32[8,64,512]{2,0,1:T(8,128)} %constant_dynamic-update-slice_fusion.1), calls=%async_computation.1 | async-start | bytes 2097152 | tf_op jit(solution)/shard_map/all_to_all | solution.py:72
  61.0 27.0 %copy-start.13 = (f32[4,32,256]{2,1,0:T(8,128)S(1)}, f32[4,32,256]{2,1,0:T(8,128)}, u32[]{:S(2)}) copy-start(f32[4,32,256]{2,1,0:T(8,128)} %param.27) | copy-start | bytes 393220
  61.7 61.3 %collective-permute-start.1 = (f32[8,4,1,256]{3,2,1,0:T(1,128)}, f32[8,4,1,256]{3,2,1,0:T(1,128)}, u32[]{:S(2)}, u32[]{:S(2)}) collective-permute-start(f32[8,4,1,256]{3,2,1,0:T(1,128)} %get-tuple-element.84), channel_id=1, source_target_pairs={{4,0},{8,4},{12,8},{16,12},{20,16},{24,20},{28,24},{32,28},{36,32}... | collective-permute-start | bytes 98312 | tf_op jit(solution)/shard_map/ppermute | solution.py:21
  64.1 58.9 %collective-permute-start.3 = (f32[8,4,1,256]{3,2,1,0:T(1,128)}, f32[8,4,1,256]{3,2,1,0:T(1,128)}, u32[]{:S(2)}, u32[]{:S(2)}) collective-permute-start(f32[8,4,1,256]{3,2,1,0:T(1,128)} %get-tuple-element.85), channel_id=1, source_target_pairs={{0,4},{4,8},{8,12},{12,16},{16,20},{20,24},{24,28},{28,32},{32,36}... | collective-permute-start | bytes 98312 | tf_op jit(solution)/shard_map/ppermute | solution.py:18
  91.7 43.0 %copy-start.1 = (f32[8,4,32,256]{3,2,1,0:T(8,128)}, f32[8,4,32,256]{3,2,1,0:T(8,128)S(1)}, u32[]{:S(2)}) copy-start(f32[8,4,32,256]{3,2,1,0:T(8,128)S(1)} %fusion.95) | copy-start | bytes 3145732
  128.1 5.6 %collective-permute-start.4 = (f32[8,4,1,256]{3,2,1,0:T(1,128)S(1)}, f32[8,4,1,256]{3,2,1,0:T(1,128)S(1)}, u32[]{:S(2)}, u32[]{:S(2)}) collective-permute-start(f32[8,4,1,256]{3,2,1,0:T(1,128)S(1)} %get-tuple-element.82), channel_id=1, source_target_pairs={{4,0},{8,4},{12,8},{16,12},{20,16},{24,20},{28,24},{32,28},{36,32}... | collective-permute-start | bytes 98312 | tf_op jit(solution)/shard_map/ppermute | solution.py:21
  130.9 3.9 collective-permute-start.5
  137.6 7.6 %collective-permute-start.6 = (f32[8,4,1,256]{3,2,1,0:T(1,128)S(1)}, f32[8,4,1,256]{3,2,1,0:T(1,128)S(1)}, u32[]{:S(2)}, u32[]{:S(2)}) collective-permute-start(f32[8,4,1,256]{3,2,1,0:T(1,128)S(1)} %get-tuple-element.80), channel_id=1, source_target_pairs={{4,0},{8,4},{12,8},{16,12},{20,16},{24,20},{28,24},{32,28},{36,32}... | collective-permute-start | bytes 98312 | tf_op jit(solution)/shard_map/ppermute | solution.py:21
  139.5 5.6 %collective-permute-start.7 = (f32[8,4,1,256]{3,2,1,0:T(1,128)S(1)}, f32[8,4,1,256]{3,2,1,0:T(1,128)S(1)}, u32[]{:S(2)}, u32[]{:S(2)}) collective-permute-start(f32[8,4,1,256]{3,2,1,0:T(1,128)S(1)} %get-tuple-element.81), channel_id=1, source_target_pairs={{0,4},{4,8},{8,12},{12,16},{16,20},{20,24},{24,28},{28,32},{32,36}... | collective-permute-start | bytes 98312 | tf_op jit(solution)/shard_map/ppermute | solution.py:18
  164.7 47.0 %all-to-all-start.2 = ((f32[8,64,512]{2,0,1:T(8,128)}), f32[8,64,512]{2,0,1:T(8,128)S(1)}, u32[]{:S(2)}, u32[]{:S(2)}) async-start(f32[8,64,512]{2,0,1:T(8,128)} %slice_dynamic-update-slice_fusion.3), calls=%async_computation.2 | async-start | bytes 2097152 | tf_op jit(solution)/shard_map/all_to_all | solution.py:65
  183.6 28.7 %copy-start.42 = (pred[3072]{0:T(1024)(128)(4,1)}, pred[3072]{0:T(1024)(128)(4,1)S(1)}, u32[]{:S(2)}) copy-start(pred[3072]{0:T(1024)(128)(4,1)S(1)} %gt.11) | copy-start | bytes 9220
  247.4 35.2 %all-to-all-start.3 = ((f32[8,64,512]{2,0,1:T(8,128)}), f32[8,64,512]{2,0,1:T(8,128)S(1)}, u32[]{:S(2)}, u32[]{:S(2)}) async-start(f32[8,64,512]{2,0,1:T(8,128)} %constant_dynamic-update-slice_fusion), calls=%async_computation.3 | async-start | bytes 2097152 | tf_op jit(solution)/shard_map/all_to_all | solution.py:72
  253.0 12.8 %collective-permute-start.10 = (f32[8,4,1,256]{3,2,1,0:T(1,128)S(1)}, f32[8,4,1,256]{3,2,1,0:T(1,128)S(1)}, u32[]{:S(2)}, u32[]{:S(2)}) collective-permute-start(f32[8,4,1,256]{3,2,1,0:T(1,128)S(1)} %get-tuple-element.78), channel_id=1, source_target_pairs={{0,4},{4,8},{8,12},{12,16},{16,20},{20,24},{24,28},{28,32},{32,36}... | collective-permute-start | bytes 98312 | tf_op jit(solution)/shard_map/ppermute | solution.py:18
  256.6 9.2 %collective-permute-start.8 = (f32[8,4,1,256]{3,2,1,0:T(1,128)S(1)}, f32[8,4,1,256]{3,2,1,0:T(1,128)S(1)}, u32[]{:S(2)}, u32[]{:S(2)}) collective-permute-start(f32[8,4,1,256]{3,2,1,0:T(1,128)S(1)} %get-tuple-element.79), channel_id=1, source_target_pairs={{4,0},{8,4},{12,8},{16,12},{20,16},{24,20},{28,24},{32,28},{36,32}... | collective-permute-start | bytes 98312 | tf_op jit(solution)/shard_map/ppermute | solution.py:21
  260.2 49.4 %collective-permute-start.11 = (f32[8,4,1,256]{3,2,1,0:T(1,128)}, f32[8,4,1,256]{3,2,1,0:T(1,128)}, u32[]{:S(2)}, u32[]{:S(2)}) collective-permute-start(f32[8,4,1,256]{3,2,1,0:T(1,128)} %get-tuple-element.77), channel_id=1, source_target_pairs={{0,4},{4,8},{8,12},{12,16},{16,20},{20,24},{24,28},{28,32},{32,36}... | collective-permute-start | bytes 98312 | tf_op jit(solution)/shard_map/ppermute | solution.py:18
  263.9 45.7 %collective-permute-start.9 = (f32[8,4,1,256]{3,2,1,0:T(1,128)}, f32[8,4,1,256]{3,2,1,0:T(1,128)}, u32[]{:S(2)}, u32[]{:S(2)}) collective-permute-start(f32[8,4,1,256]{3,2,1,0:T(1,128)} %get-tuple-element.76), channel_id=1, source_target_pairs={{4,0},{8,4},{12,8},{16,12},{20,16},{24,20},{28,24},{32,28},{36,32}... | collective-permute-start | bytes 98312 | tf_op jit(solution)/shard_map/ppermute | solution.py:21
  315.1 5.6 %collective-permute-start.12 = (f32[8,4,1,256]{3,2,1,0:T(1,128)S(1)}, f32[8,4,1,256]{3,2,1,0:T(1,128)S(1)}, u32[]{:S(2)}, u32[]{:S(2)}) collective-permute-start(f32[8,4,1,256]{3,2,1,0:T(1,128)S(1)} %get-tuple-element.74), channel_id=1, source_target_pairs={{4,0},{8,4},{12,8},{16,12},{20,16},{24,20},{28,24},{32,28},{36,32}... | collective-permute-start | bytes 98312 | tf_op jit(solution)/shard_map/ppermute | solution.py:21
  317.1 4.5 %collective-permute-start.13 = (f32[8,4,1,256]{3,2,1,0:T(1,128)S(1)}, f32[8,4,1,256]{3,2,1,0:T(1,128)S(1)}, u32[]{:S(2)}, u32[]{:S(2)}) collective-permute-start(f32[8,4,1,256]{3,2,1,0:T(1,128)S(1)} %get-tuple-element.75), channel_id=1, source_target_pairs={{0,4},{4,8},{8,12},{12,16},{16,20},{20,24},{24,28},{28,32},{32,36}... | collective-permute-start | bytes 98312 | tf_op jit(solution)/shard_map/ppermute | solution.py:18
  323.8 6.2 %collective-permute-start.14 = (f32[8,4,1,256]{3,2,1,0:T(1,128)S(1)}, f32[8,4,1,256]{3,2,1,0:T(1,128)S(1)}, u32[]{:S(2)}, u32[]{:S(2)}) collective-permute-start(f32[8,4,1,256]{3,2,1,0:T(1,128)S(1)} %get-tuple-element.72), channel_id=1, source_target_pairs={{4,0},{8,4},{12,8},{16,12},{20,16},{24,20},{28,24},{32,28},{36,32}... | collective-permute-start | bytes 98312 | tf_op jit(solution)/shard_map/ppermute | solution.py:21
  325.7 5.3 %collective-permute-start.15 = (f32[8,4,1,256]{3,2,1,0:T(1,128)S(1)}, f32[8,4,1,256]{3,2,1,0:T(1,128)S(1)}, u32[]{:S(2)}, u32[]{:S(2)}) collective-permute-start(f32[8,4,1,256]{3,2,1,0:T(1,128)S(1)} %get-tuple-element.73), channel_id=1, source_target_pairs={{0,4},{4,8},{8,12},{12,16},{16,20},{20,24},{24,28},{28,32},{32,36}... | collective-permute-start | bytes 98312 | tf_op jit(solution)/shard_map/ppermute | solution.py:18
  347.8 44.4 %copy-start.43 = (pred[3072]{0:T(1024)(128)(4,1)S(1)}, pred[3072]{0:T(1024)(128)(4,1)}, u32[]{:S(2)}) copy-start(pred[3072]{0:T(1024)(128)(4,1)} %copy-done.42) | copy-start | bytes 9220
  (42 other events, 457.2 us)
where the time goes:
time: 415 us; the launch traced here: 413 us
  other arithmetic  135 us (33%)
  starting transfers between devices  94.5 us (23%)
  local copies, waits for them, and re-layouts  91.8 us (22%)
  waiting for transfers between devices  45.5 us (11%)
  blocking collectives  44.3 us (11%)
    all_to_all x1, blocking collectives, forward_leakage(): lax.all_to_all(outgoing, 'space', split_axis=1, concat_axis=1, tiled=True)  44.3 us
    scatter-add x2, other arithmetic, body(): river_rhs.at[:, columns].add((weight[None] * fetched).reshape(members, -1))  42.2 us
    scatter-add x2, other arithmetic, body(): jnp.zeros((members, reach_count), jnp.float32).at[:, owner_ids]  38.3 us
    ppermute x8, starting transfers between devices, padded_2(): lax.ppermute(lax.slice_in_dim(block, block.shape[dim] - width, None, axis...  28.5 us
    all_to_all x1, waiting for transfers between devices, forward_leakage(): lax.all_to_all(outgoing, 'space', split_axis=1, concat_axis=1, tiled=True)  28.1 us
    gather x2, local copies, waits for them, and re-layouts, body(): reply = section_now[:, owner_ids].reshape(members, bucket_count, -1)  22.8 us
    gather x2, local copies, waits for them, and re-layouts, body(): head_now[:, 0].reshape(members, -1)[:, columns]  20.6 us
    all_to_all x1, starting transfers between devices, forward_leakage(): lax.all_to_all(outgoing, 'space', split_axis=1, concat_axis=1, tiled=True)  18.8 us
  transfers between devices with their start and end apart: 20, of which 6 were waited for; matrix products, arithmetic and copies ran while one was open for 28% of the time, Pallas kernels for 0%

commit v1 on v0

v1 whole, which is shorter than its diff:
```python
import functools

import jax
import jax.numpy as jnp
from jax import lax
from jax.experimental import pallas as pl
from jax.experimental.pallas import tpu as pltpu
from jax.sharding import PartitionSpec as P

PICARD = 2
SWEEPS = 3
NEAR = 2
FAR = 2 * NEAR + 1
LANES = 128
F32 = jnp.float32
BF16 = jnp.bfloat16


def harmonic(first, second):
    return 2.0 * first * second / (first + second)


def halves(values):
    high = values.astype(BF16)
    return high, (values - high.astype(F32)).astype(BF16)


def dot_rows(left, right):
    return lax.dot_general(left, right, (((1,), (1,)), ((), ())), preferred_element_type=F32)


def kernel(
    tile_count,
    head_in, recharge_in, section_in, inflow_in, soil_in, class_conduct, class_alpha,
    capacity_in, cell_in, reach_in, cond_in, rate_in,
    head_out, section_out,
    stage, recharge, section, inflow, soil, capacity, cell, reach, cond, rate,
    heads, kc, ka, base, source, face_x, face_y, face_z, inverse, col_cond,
    one_y, mask_x, one_r, weight, fetched, leak, river,
    edge, edge_got, sect0, sect1, part1, part2, got1, got2, partial_state, state_got, rate_got,
    load_sem, store_sem, halo_send, halo_recv, edge_send, edge_recv,
    sect_send, sect_recv, leak_send, leak_recv, state_send, state_recv, rate_send, rate_recv,
):
    me = lax.axis_index("space")
    layers, padded, members, width = heads.shape[1:]
    rows = padded - 2
    buckets, slots = cell.shape
    groups = section.shape[1] // LANES
    near = [bucket for bucket in range(buckets) if bucket not in (NEAR, FAR)]
    remote = near + [FAR]

    def tile(shift):
        return lax.rem(me + shift + tile_count, tile_count)

    def user(bucket):
        return tile(tile_count // 2 if bucket == FAR else NEAR - bucket)

    def owner(bucket):
        return tile(tile_count // 2 if bucket == FAR else bucket - NEAR)

    def send(source_ref, target_ref, send_sem, recv_sem, device):
        return pltpu.make_async_remote_copy(
            src_ref=source_ref, dst_ref=target_ref, send_sem=send_sem, recv_sem=recv_sem,
            device_id={"space": device}, device_id_type=pl.DeviceIdType.MESH)

    loads = {}
    pairs = [("section", section_in, section), ("rate", rate_in, rate), ("soil", soil_in, soil)]
    for half in range(2):
        lanes = pl.ds(half * LANES, LANES)
        pairs.append(("head%d" % half, head_in.at[:, lanes], stage.at[half]))
        pairs.append(("recharge%d" % half, recharge_in.at[:, lanes], recharge.at[half]))
    pairs += [("capacity", capacity_in, capacity), ("cell", cell_in, cell), ("reach", reach_in, reach),
              ("cond", cond_in, cond), ("inflow", inflow_in, inflow)]
    for index, (name, source_ref, target_ref) in enumerate(pairs):
        loads[name] = pltpu.make_async_copy(source_ref, target_ref, load_sem.at[index])
        loads[name].start()

    barrier = pltpu.get_barrier_semaphore()
    for bucket in remote:
        pl.semaphore_signal(barrier, inc=1, device_id={"space": user(bucket)},
                            device_id_type=pl.DeviceIdType.MESH)
    pl.semaphore_wait(barrier, len(remote))

    sends = []
    loads["section"].wait()
    loads["rate"].wait()
    first_sections = {}
    for bucket in [FAR] + near:
        copy = send(section, sect0.at[bucket], sect_send.at[0, bucket], sect_recv.at[0, bucket], user(bucket))
        copy.start()
        first_sections[bucket] = copy
        sends.append(copy)
    rate_copy = send(rate, rate_got, rate_send, rate_recv, user(FAR))
    rate_copy.start()
    sends.append(rate_copy)

    loads["soil"].wait()
    classes = soil[...]
    conduct_of = jnp.zeros(classes.shape, F32)
    alpha_of = jnp.zeros(classes.shape, F32)
    for index in range(class_conduct.shape[0]):
        match = classes == index
        conduct_of = jnp.where(match, class_conduct[index], conduct_of)
        alpha_of = jnp.where(match, class_alpha[index], alpha_of)
    kc[:, 1:rows + 1, :] = conduct_of
    ka[:, 1:rows + 1, :] = alpha_of
    for side, row in ((0, 0), (1, rows - 1)):
        for layer in range(layers):
            edge[side, layer:layer + 1, :] = conduct_of[layer, row:row + 1, :]
            edge[side, layers + layer:layers + layer + 1, :] = alpha_of[layer, row:row + 1, :]
    edge_copies = []
    for side, shift in ((0, -1), (1, 1)):
        copy = send(edge.at[side], edge_got.at[1 - side], edge_send.at[side], edge_recv.at[1 - side], tile(shift))
        copy.start()
        edge_copies.append(copy)
        sends.append(copy)

    def halo(index):
        copies = [
            send(heads.at[index, :, 1], heads.at[index, :, rows + 1],
                 halo_send.at[index, 0], halo_recv.at[index, 1], tile(-1)),
            send(heads.at[index, :, rows], heads.at[index, :, 0],
                 halo_send.at[index, 1], halo_recv.at[index, 0], tile(1)),
        ]
        for copy in copies:
            copy.start()
        sends.extend(copies)
        return copies

    for half in range(2):
        loads["head%d" % half].wait()
        loads["recharge%d" % half].wait()
    loads["capacity"].wait()

    def begin(x):
        for layer in range(layers):
            cap = capacity[layer, pl.ds(x, 1), :]
            for half in range(2):
                lanes = slice(half * LANES, (half + 1) * LANES)
                value = stage[half, pl.ds(layer * rows + x, members, stride=layers * rows), :]
                heads[0, layer, x + 1, :, lanes] = value
                term = cap[:, lanes] * value
                if layer == 0:
                    term = term + recharge[half, pl.ds(x, members, stride=rows), :]
                base[layer, x, :, lanes] = term

    def over(start, stop, body):
        def step(x, carry):
            body(x)
            return carry
        lax.fori_loop(start, stop, step, 0)

    begin(0)
    begin(rows - 1)
    halos = halo(0)
    over(1, rows - 1, begin)

    loads["cell"].wait()
    loads["reach"].wait()
    loads["cond"].wait()
    live = reach[...] >= 0
    columns = jnp.where(live, cell[...], 0)
    reaches = jnp.where(live, reach[...], 0)
    weight[...] = jnp.where(live, cond[...], 0.0)
    column_x = columns // width
    column_y = columns % width
    reach_high = reaches // LANES
    reach_low = reaches % LANES
    ids = lax.broadcasted_iota(jnp.int32, (width, slots), 0)
    total = jnp.zeros((2 * rows, width), F32)
    for bucket in range(buckets):
        own = slice(bucket, bucket + 1)
        one_y[bucket] = (ids == column_y[own]).astype(F32).astype(BF16)
        mask_x[bucket] = (ids // members == column_x[own]).astype(F32).astype(BF16)
        one_r[bucket] = (ids % LANES == reach_low[own]).astype(F32).astype(BF16)
        terms = jnp.where(ids[:rows] == column_x[own], weight[own, :], 0.0)
        total = total + dot_rows(jnp.concatenate(halves(terms), axis=0), one_y[bucket])
    col_cond[...] = total[:rows] + total[rows:]

    for copy in edge_copies:
        copy.wait_recv()
    for side, row, outside in ((0, 0, 0), (1, rows + 1, tile_count - 1)):
        inside = jnp.where(me == outside, 0.0, 1.0)
        for layer in range(layers):
            kc[layer, row:row + 1, :] = edge_got[side, layer:layer + 1, :] * inside
            ka[layer, row:row + 1, :] = edge_got[side, layers + layer:layers + layer + 1, :]

    lane = lax.broadcasted_iota(jnp.int32, (members, width), 1)

    def conduct(index, x):
        return tuple(
            kc[layer, pl.ds(x, 1), :]
            * jnp.exp(ka[layer, pl.ds(x, 1), :] * jnp.minimum(heads[index, layer, x], 0.0))
            for layer in range(layers))

    def link(index):
        low = conduct(index, 0)
        here = conduct(index, 1)
        before = tuple(harmonic(a, b) for a, b in zip(low, here))
        for layer in range(layers):
            face_x[layer, 0] = before[layer]

        def step(x, carry):
            here, before = carry
            after = conduct(index, x + 1)
            ahead = tuple(harmonic(a, b) for a, b in zip(here, after))
            down = None
            for layer in range(layers):
                face_x[layer, x] = ahead[layer]
                along = harmonic(here[layer], pltpu.roll(here[layer], width - 1, 1))
                along = jnp.where(lane == width - 1, 0.0, along)
                face_y[layer, x - 1] = along
                diagonal = capacity[layer, pl.ds(x - 1, 1), :] + ahead[layer] + before[layer]
                diagonal = diagonal + along + pltpu.roll(along, 1, 1)
                if layer > 0:
                    diagonal = diagonal + down
                if layer < layers - 1:
                    down = 0.5 * harmonic(here[layer], here[layer + 1])
                    face_z[layer, x - 1] = down
                    diagonal = diagonal + down
                if layer == 0:
                    diagonal = diagonal + col_cond[pl.ds(x - 1, 1), :]
                inverse[layer, x - 1] = 1.0 / diagonal
            return after, ahead

        lax.fori_loop(1, rows + 1, step, (here, before))

    def relax(index, x):
        now = [heads[index, layer, x] for layer in range(layers)]
        results = []
        for layer in range(layers):
            along = face_y[layer, x - 1]
            total = source[x - 1] if layer == 0 else base[layer, x - 1]
            total = total + face_x[layer, x] * heads[index, layer, x + 1]
            total = total + face_x[layer, x - 1] * heads[index, layer, x - 1]
            total = total + along * pltpu.roll(now[layer], width - 1, 1)
            total = total + pltpu.roll(along * now[layer], 1, 1)
            if layer < layers - 1:
                total = total + face_z[layer, x - 1] * now[layer + 1]
            if layer > 0:
                total = total + face_z[layer - 1, x - 1] * now[layer - 1]
            results.append(total * inverse[layer, x - 1])
        return results

    def sweep(index, last):
        def body(x):
            results = relax(index, x)
            for layer in range(layers):
                if layer == 0 or not last:
                    heads[index + 1, layer, x] = results[layer]
                if last:
                    for half in range(2):
                        stage[half, pl.ds(layer * rows + x - 1, members, stride=layers * rows), :] = (
                            results[layer][:, half * LANES:(half + 1) * LANES])
        if last:
            over(1, rows + 1, body)
            return None
        body(1)
        body(rows)
        copies = halo(index + 1)
        over(2, rows, body)
        return copies

    def by_group(values):
        return jnp.concatenate([values[:, g * LANES:(g + 1) * LANES] for g in range(groups)], axis=0)

    def river_term(sections):
        total = jnp.zeros((2 * rows * members, width), F32)
        for bucket in [NEAR] + remote:
            own = slice(bucket, bucket + 1)
            left = jnp.concatenate(halves(by_group(sections(bucket))), axis=1)
            picked = jnp.dot(left, one_r[bucket], preferred_element_type=F32)
            value = jnp.zeros((members, slots), F32)
            for g in range(groups):
                value = value + jnp.where(reach_high[own] == g, picked[g * members:(g + 1) * members], 0.0)
            fetched[bucket] = value
            flow = weight[own, :] * value
            terms = halves(jnp.concatenate([flow, flow], axis=0))
            spread = [mask_x[bucket] * jnp.concatenate([term] * (rows // 2), axis=0) for term in terms]
            total = total + dot_rows(jnp.concatenate(spread, axis=0), one_y[bucket])
        river[...] = (total[:rows * members] + total[rows * members:]).reshape(rows, members, width)

    def leak_parts(index, parts):
        top = heads[index, 0, 1:rows + 1].reshape(rows * members, width)
        terms = halves(top)
        for bucket in [FAR] + near + [NEAR]:
            own = slice(bucket, bucket + 1)
            picked = jnp.dot(terms[0], one_y[bucket], preferred_element_type=F32)
            picked = picked + jnp.dot(terms[1], one_y[bucket], preferred_element_type=F32)
            value = jnp.zeros((members, slots), F32)
            for x in range(rows):
                value = value + jnp.where(column_x[own] == x, picked[x * members:(x + 1) * members], 0.0)
            flow = weight[own, :] * (fetched[bucket] - value)
            spread = jnp.concatenate([jnp.where(reach_high[own] == g, flow, 0.0) for g in range(groups)], axis=0)
            sums = dot_rows(jnp.concatenate(halves(spread), axis=0), one_r[bucket, :LANES, :])
            sums = sums[:groups * members] + sums[groups * members:]
            for g in range(groups):
                parts[bucket, :, g * LANES:(g + 1) * LANES] = sums[g * members:(g + 1) * members]

    def send_parts(step, parts, got):
        copies = {}
        for bucket in [FAR] + near:
            copy = send(parts.at[bucket], got.at[bucket], leak_send.at[step, bucket],
                        leak_recv.at[step, bucket], owner(bucket))
            copy.start()
            copies[bucket] = copy
            sends.append(copy)
        return copies

    def near_state(parts, got):
        values = parts[NEAR]
        for bucket in near:
            values = values + got[bucket]
        return values

    def with_rate(rates, values):
        return jnp.concatenate(
            [rates[g:g + 1, :] * values[:, g * LANES:(g + 1) * LANES] for g in range(groups)], axis=1)

    for copy in halos:
        copy.wait_recv()
    link(0)
    for bucket in [FAR] + near:
        first_sections[bucket].wait_recv()
    river_term(lambda bucket: section[...] if bucket == NEAR else sect0[bucket])
    source[...] = base[0] + river[...]
    index = 0
    for sweep_index in range(SWEEPS):
        if sweep_index > 0:
            for copy in halos:
                copy.wait_recv()
        halos = sweep(index, False)
        index += 1
    leak_parts(index, part1)
    copies = send_parts(0, part1, got1)
    for copy in halos:
        copy.wait_recv()
    link(index)

    loads["inflow"].wait()
    rate_copy.wait_recv()
    for bucket in near:
        copies[bucket].wait_recv()
    partial_state[...] = section[...] + with_rate(rate, inflow[...] - near_state(part1, got1))
    state_copy = send(partial_state, state_got, state_send, state_recv, user(FAR))
    state_copy.start()
    sends.append(state_copy)
    copies[FAR].wait_recv()
    sect1[NEAR] = partial_state[...] - with_rate(rate, got1[FAR])
    second_sections = []
    for bucket in near:
        copy = send(sect1.at[NEAR], sect1.at[bucket], sect_send.at[1, bucket], sect_recv.at[1, bucket], user(bucket))
        copy.start()
        second_sections.append(copy)
        sends.append(copy)
    state_copy.wait_recv()
    sect1[FAR] = state_got[...] - with_rate(rate_got, part1[FAR])
    for copy in second_sections:
        copy.wait_recv()

    river_term(lambda bucket: sect1[bucket])
    source[...] = base[0] + river[...]
    for sweep_index in range(SWEEPS):
        if sweep_index > 0:
            for copy in halos:
                copy.wait_recv()
        halos = sweep(index, sweep_index == SWEEPS - 1)
        index += 1
    stores = []
    for half in range(2):
        copy = pltpu.make_async_copy(stage.at[half], head_out.at[:, pl.ds(half * LANES, LANES)], store_sem.at[half])
        copy.start()
        stores.append(copy)
    leak_parts(index, part2)
    copies = send_parts(1, part2, got2)
    for bucket in remote:
        copies[bucket].wait_recv()
    values = near_state(part2, got2) + got2[FAR]
    leak[...] = section[...] + with_rate(rate, inflow[...] - values)
    copy = pltpu.make_async_copy(leak, section_out, store_sem.at[2])
    copy.start()
    stores.append(copy)
    for copy in stores:
        copy.wait()
    for copy in sends:
        copy.wait_send()


def body(tile_count, head_start, recharge, section_start, inflow, soil_class, class_conduct, class_alpha,
         capacity, river_cell, river_reach, river_cond, reach_rate):
    members, layers, rows, width = head_start.shape
    buckets, slots = river_cell.shape[1:]
    reaches = section_start.shape[1]
    groups = reaches // LANES
    any_spec = pl.BlockSpec(memory_space=pl.ANY)
    smem_spec = pl.BlockSpec(memory_space=pltpu.SMEM)
    vmem = pltpu.VMEM
    grid = (layers, rows, members, width)
    state = (members, reaches)
    scratch = [
        vmem((2, members * layers * rows, LANES), F32), vmem((2, members * rows, LANES), F32),
        vmem(state, F32), vmem(state, F32), vmem((layers, rows, width), jnp.int32), vmem((layers, rows, width), F32),
        vmem((buckets, slots), jnp.int32), vmem((buckets, slots), jnp.int32), vmem((buckets, slots), F32),
        vmem((groups, LANES), F32),
        vmem((PICARD * SWEEPS + 1, layers, rows + 2, members, width), F32),
        vmem((layers, rows + 8, width), F32), vmem((layers, rows + 8, width), F32),
        vmem(grid, F32), vmem((rows, members, width), F32),
        vmem((layers, rows + 1, members, width), F32), vmem(grid, F32),
        vmem((layers - 1, rows, members, width), F32), vmem(grid, F32), vmem((rows, width), F32),
        vmem((buckets, width, slots), BF16), vmem((buckets, rows * members, slots), BF16),
        vmem((buckets, 2 * LANES, slots), BF16),
        vmem((buckets, slots), F32), vmem((buckets, members, slots), F32), vmem(state, F32),
        vmem((rows, members, width), F32),
        vmem((2, 2 * layers, width), F32), vmem((2, 2 * layers, width), F32),
    ] + [vmem((buckets,) + state, F32)] * 6 + [vmem(state, F32)] * 2 + [vmem((groups, LANES), F32)] + [
        pltpu.SemaphoreType.DMA((12,)), pltpu.SemaphoreType.DMA((3,)),
        pltpu.SemaphoreType.DMA((PICARD * SWEEPS, 2)), pltpu.SemaphoreType.DMA((PICARD * SWEEPS, 2)),
        pltpu.SemaphoreType.DMA((2,)), pltpu.SemaphoreType.DMA((2,)),
        pltpu.SemaphoreType.DMA((2, buckets)), pltpu.SemaphoreType.DMA((2, buckets)),
        pltpu.SemaphoreType.DMA((2, buckets)), pltpu.SemaphoreType.DMA((2, buckets)),
        pltpu.SemaphoreType.DMA, pltpu.SemaphoreType.DMA, pltpu.SemaphoreType.DMA, pltpu.SemaphoreType.DMA,
    ]
    head, section = pl.pallas_call(
        functools.partial(kernel, tile_count),
        out_shape=(jax.ShapeDtypeStruct((members * layers * rows, width), F32),
                   jax.ShapeDtypeStruct(state, F32)),
        in_specs=[any_spec] * 5 + [smem_spec] * 2 + [any_spec] * 5,
        out_specs=(any_spec, any_spec),
        scratch_shapes=scratch,
        compiler_params=pltpu.CompilerParams(
            collective_id=0, has_side_effects=True, vmem_limit_bytes=60 * 1024 * 1024),
        name="aquifer",
    )(head_start.reshape(-1, width), recharge.reshape(-1, width), section_start, inflow, soil_class,
      class_conduct, class_alpha, capacity, river_cell[0], river_reach[0], river_cond[0],
      reach_rate.reshape(groups, LANES))
    return head.reshape(head_start.shape), section


def solution(mesh):
    return jax.shard_map(
        functools.partial(body, mesh.shape["space"]),
        mesh=mesh,
        in_specs=(
            P("member", None, "space", None),
            P("member", "space", None),
            P("member", "space"),
            P("member", "space"),
            P(None, "space", None),
            P(),
            P(),
            P(None, "space", None),
            P("space", None, None),
            P("space", None, None),
            P("space", None, None),
            P("space"),
        ),
        out_specs=(P("member", None, "space", None), P("member", "space")),
        check_vma=False,
    )
```

time: 415 us -> 74.7 us (0.18)
  other arithmetic: 135 us -> 0 us
  starting transfers between devices: 94.5 us -> 0 us
  local copies, waits for them, and re-layouts: 91.8 us -> 4.87 us
  Pallas kernels: 0 us -> 68.9 us
  waiting for transfers between devices: 45.5 us -> 0 us
  blocking collectives: 44.3 us -> 0 us
    scatter-add x9 -> x0, other arithmetic: 101 us -> none  [the longest x2 42.2 us: body(): river_rhs.at[:, columns].add((weight[None] * fetched).reshape(members, -1))]
    pallas_call x0 -> x1, Pallas kernels: none -> 68.9 us  [body(): pl.pallas_call(functools.partial(kernel, tile_count), out_shape=(jax.Shap...]
    all_to_all x4 -> x0, starting transfers between devices: 48.8 us -> none  [the longest x1 18.8 us: forward_leakage(): lax.all_to_all(outgoing, 'space', split_axis=1, concat_axis=1, tiled=True)]
    ppermute x16 -> x0, starting transfers between devices: 45.7 us -> none  [the longest x8 28.5 us: padded_2(): lax.ppermute(lax.slice_in_dim(block, block.shape[dim] - width, None, axis...]
    all_to_all x1 -> x0, blocking collectives: 44.3 us -> none  [forward_leakage(): lax.all_to_all(outgoing, 'space', split_axis=1, concat_axis=1, tiled=True)]
    gather x4 -> x0, local copies, waits for them, and re-layouts: 43.5 us -> none  [the longest x2 22.8 us: body(): reply = section_now[:, owner_ids].reshape(members, bucket_count, -1)]
    all_to_all x4 -> x0, waiting for transfers between devices: 42.5 us -> none  [the longest x1 28.1 us: forward_leakage(): lax.all_to_all(outgoing, 'space', split_axis=1, concat_axis=1, tiled=True)]
    slice x21 -> x0, local copies, waits for them, and re-layouts: 19.1 us -> none  [the longest x4 5.34 us: body(): head_now[:, 0].reshape(members, -1)[:, columns]]
  transfers between devices with their start and end apart: 20 -> 0, of which waited for: 6 -> 0; matrix products, arithmetic and copies ran while one was open for 28% -> 0% of each run, Pallas kernels for 0% -> 0%
where the time goes in v1:
time: 74.7 us; the launch traced here: 74.5 us
  Pallas kernels  68.9 us (92%)
  local copies, waits for them, and re-layouts  4.87 us (7%)
    pallas_call x1, Pallas kernels, body(): pl.pallas_call(functools.partial(kernel, tile_count), out_shape=(jax.Shap...  68.9 us
    unnamed x10, local copies, waits for them, and re-layouts  4.87 us

profile of v1, /device:TPU:1, one launch (start us, length us, event | category | flops | bytes accessed | tf_op | source)
XLA Modules:
  0.0 74.5 jit_solution(7120999845095722951)
XLA Ops:
  0.6 0.0 copy-start.1
  0.6 0.0 copy-start.2
  0.7 1.3 %copy.20 = f32[1,6,512]{2,1,0:T(8,128)} copy(f32[1,6,512]{2,0,1:T(1,128)} %param.22) | data formatting | bytes 24576
  2.0 0.0 copy-done.1
  2.0 0.0 copy-done.2
  2.0 0.6 copy_bitcast_fusion.1
  2.6 68.9 %aquifer.1 = (f32[1024,256]{1,0:T(8,128)}, f32[8,1024]{1,0:T(8,128)}) custom-call(f32[1024,256]{1,0:T(8,128)} %bitcast.11, f32[256,256]{1,0:T(8,128)} %bitcast.13, f32[8,1024]{1,0:T(8,128)} %section_in.1, f32[8,1024]{1,0:T(8,128)} %inflow_in.1, s32[4,32,256]{2,1,0:T(8,128)} %soil_in.1, f32[12]{0:T(128)} %class_conduct.1, f32[12]{0:T(128)} %class_alpha.1, ...), custom_call_target="tpu_custom_call" | custom-call | tf_op jit(solution)/shard_map/aquifer/pallas_call | solution.py:423
  71.5 0.0 copy-start
  71.5 2.3 %copy.23 = f32[8,4,32,256]{3,2,1,0:T(8,128)} copy(f32[8,4,32,256]{3,2,1,0:T(8,128)} %bitcast.12) | data formatting | bytes 2097152
  73.8 0.0 copy-done
  73.8 0.6 copy.24
Async XLA Ops:
  0.6 1.3 %copy-start.1 = (s32[1,6,512]{2,0,1:T(1,128)S(1)}, s32[1,6,512]{2,0,1:T(1,128)}, u32[]{:S(2)}) copy-start(s32[1,6,512]{2,0,1:T(1,128)} %param.21) | copy-start | bytes 36868
  0.6 1.3 %copy-start.2 = (s32[1,6,512]{2,0,1:T(1,128)S(1)}, s32[1,6,512]{2,0,1:T(1,128)}, u32[]{:S(2)}) copy-start(s32[1,6,512]{2,0,1:T(1,128)} %param.20) | copy-start | bytes 36868
  71.5 2.3 %copy-start = (f32[8,1024]{1,0:T(8,128)S(1)}, f32[8,1024]{1,0:T(8,128)}, u32[]{:S(2)}) copy-start(f32[8,1024]{1,0:T(8,128)} %get-tuple-element.11) | copy-start | bytes 98308

commit v2 on v1

v2 whole, which is shorter than its diff:
```python
import functools

import jax
import jax.numpy as jnp
from jax import lax
from jax.experimental import pallas as pl
from jax.experimental.pallas import tpu as pltpu
from jax.sharding import PartitionSpec as P

PICARD = 2
SWEEPS = 3
NEAR = 2
FAR = 2 * NEAR + 1
LANES = 128
F32 = jnp.float32
BF16 = jnp.bfloat16


def halves(values):
    high = values.astype(BF16)
    return high, (values - high.astype(F32)).astype(BF16)


def dot_rows(left, right):
    return lax.dot_general(left, right, (((1,), (1,)), ((), ())), preferred_element_type=F32)


def kernel(
    tile_count,
    head_in, recharge_in, section_in, inflow_in, soil_in, class_conduct, class_alpha,
    capacity_in, cell_in, reach_in, cond_in, rate_in,
    head_out, section_out,
    head0, head1, head2, head3, head4, head5, head6,
    recharge, section, inflow, soil, capacity, cell, reach, cond, rate,
    kc, ka, base, source, face_x, face_y, face_z, inverse, col_cond,
    one_y, mask_x, one_r, spread, weight, column_x, column_y, reach_high, reach_low, fetched, river,
    edge, edge_got, sect0, sect1, part1, part2, got1, got2, partial_state, state_got, rate_got,
    load_sem, head_sem, recharge_sem, store_sem, halo_send, halo_recv, edge_send, edge_recv,
    sect_send, sect_recv, leak_send, leak_recv, state_send, state_recv, rate_send, rate_recv,
):
    me = lax.axis_index("space")
    heads = (head0, head1, head2, head3, head4, head5, head6)
    layers, padded, members, width = head0.shape
    rows = padded - 2
    buckets, slots = weight.shape
    pieces = slots // LANES
    groups = section.shape[1] // LANES
    near = [bucket for bucket in range(buckets) if bucket not in (NEAR, FAR)]
    remote = near + [FAR]

    def tile(shift):
        return lax.rem(me + shift + tile_count, tile_count)

    def user(bucket):
        return tile(tile_count // 2 if bucket == FAR else NEAR - bucket)

    def owner(bucket):
        return tile(tile_count // 2 if bucket == FAR else bucket - NEAR)

    def own(bucket):
        return slice(bucket, bucket + 1)

    def slot_range(bucket):
        return slice(bucket * slots, (bucket + 1) * slots)

    sends = []

    def send(source_ref, target_ref, send_sem, recv_sem, device):
        copy = pltpu.make_async_remote_copy(
            src_ref=source_ref, dst_ref=target_ref, send_sem=send_sem, recv_sem=recv_sem,
            device_id={"space": device}, device_id_type=pl.DeviceIdType.MESH)
        copy.start()
        sends.append(copy)
        return copy

    def over(start, stop, size, body):
        def step(count, carry):
            body([start + count * size + offset for offset in range(size)])
            return carry
        lax.fori_loop(0, (stop - start) // size, step, 0)

    loads = {}
    pairs = [("soil", soil_in, soil), ("section", section_in, section), ("rate", rate_in, rate),
             ("cell", cell_in, cell), ("reach", reach_in, reach), ("cond", cond_in, cond)]
    for index, (name, source_ref, target_ref) in enumerate(pairs):
        loads[name] = pltpu.make_async_copy(source_ref, target_ref, load_sem.at[index])
        loads[name].start()
    head_loads = [pltpu.make_async_copy(head_in.at[m], head0.at[:, 1:rows + 1, m, :], head_sem.at[m])
                  for m in range(members)]
    for copy in head_loads:
        copy.start()
    for index, (name, source_ref, target_ref) in enumerate(
            [("capacity", capacity_in, capacity), ("inflow", inflow_in, inflow)]):
        loads[name] = pltpu.make_async_copy(source_ref, target_ref, load_sem.at[len(pairs) + index])
        loads[name].start()
    recharge_loads = [pltpu.make_async_copy(recharge_in.at[m], recharge.at[:, m, :], recharge_sem.at[m])
                      for m in range(members)]
    for copy in recharge_loads:
        copy.start()

    barrier = pltpu.get_barrier_semaphore()
    for bucket in remote:
        pl.semaphore_signal(barrier, inc=1, device_id={"space": user(bucket)},
                            device_id_type=pl.DeviceIdType.MESH)

    loads["soil"].wait()
    classes = soil[...]
    conduct_of = jnp.zeros(classes.shape, F32)
    alpha_of = jnp.zeros(classes.shape, F32)
    for index in range(class_conduct.shape[0]):
        match = classes == index
        conduct_of = jnp.where(match, 2.0 * class_conduct[index], conduct_of)
        alpha_of = jnp.where(match, class_alpha[index], alpha_of)
    kc[:, 1:rows + 1, :] = conduct_of
    ka[:, 1:rows + 1, :] = alpha_of
    for side, row in ((0, 0), (1, rows - 1)):
        for layer in range(layers):
            edge[side, layer:layer + 1, :] = conduct_of[layer, row:row + 1, :]
            edge[side, layers + layer:layers + layer + 1, :] = alpha_of[layer, row:row + 1, :]

    loads["cell"].wait()
    loads["reach"].wait()
    loads["cond"].wait()
    live = reach[...] >= 0
    columns = jnp.where(live, cell[...], 0)
    reaches = jnp.where(live, reach[...], 0)
    for target_ref, values in (
            (weight, jnp.where(live, cond[...], 0.0)),
            (column_x, columns // width), (column_y, columns % width),
            (reach_high, reaches // LANES), (reach_low, reaches % LANES)):
        for bucket in range(buckets):
            for piece in range(pieces):
                line = bucket * pieces + piece
                target_ref[own(bucket), piece * LANES:(piece + 1) * LANES] = (
                    values[line:line + 1, :].astype(F32))

    def one_hot(ids, row):
        rows16 = jnp.broadcast_to(row, (16, slots)).astype(BF16)
        wide = jnp.concatenate([rows16] * (ids.shape[0] // 16), axis=0)
        return jnp.where(ids == wide, jnp.ones((), BF16), jnp.zeros((), BF16))

    ids = lax.broadcasted_iota(jnp.int32, (width, slots), 0)
    y_ids = ids.astype(F32).astype(BF16)
    x_ids = (ids // members).astype(F32).astype(BF16)
    r_ids = (ids % LANES).astype(F32).astype(BF16)

    def build(bucket):
        wide = slot_range(bucket)
        values = one_hot(y_ids, column_y[own(bucket), :])
        one_y[:width, wide] = values
        one_y[width:, wide] = values
        mask_x[:, wide] = one_hot(x_ids, column_x[own(bucket), :])
        one_r[:, wide] = one_hot(r_ids, reach_low[own(bucket), :])

    build(0)
    build(1)
    build(2)

    pl.semaphore_wait(barrier, len(remote))

    loads["section"].wait()
    loads["rate"].wait()
    first_sections = {}
    for bucket in [FAR] + near:
        first_sections[bucket] = send(
            section, sect0.at[bucket], sect_send.at[0, bucket], sect_recv.at[0, bucket], user(bucket))
    rate_copy = send(rate, rate_got, rate_send, rate_recv, user(FAR))
    edge_copies = [
        send(edge.at[side], edge_got.at[1 - side], edge_send.at[side], edge_recv.at[1 - side], tile(shift))
        for side, shift in ((0, -1), (1, 1))]

    def halo(index):
        return [
            send(heads[index].at[:, 1], heads[index].at[:, rows + 1],
                 halo_send.at[index, 0], halo_recv.at[index, 1], tile(-1)),
            send(heads[index].at[:, rows], heads[index].at[:, 0],
                 halo_send.at[index, 1], halo_recv.at[index, 0], tile(1)),
        ]

    for copy in head_loads:
        copy.wait()
    halos = halo(0)

    for bucket in range(3, buckets):
        build(bucket)
    flat = lax.broadcasted_iota(jnp.int32, (rows, slots), 0).astype(F32)
    total = jnp.zeros((2 * rows, width), F32)
    for bucket in range(buckets):
        terms = jnp.where(flat == column_x[own(bucket), :], weight[own(bucket), :], 0.0)
        total = total + dot_rows(jnp.concatenate(halves(terms), axis=0), one_y[:width, slot_range(bucket)])
    col_cond[...] = total[:rows] + total[rows:]

    loads["capacity"].wait()
    for copy in recharge_loads:
        copy.wait()

    def begin(block):
        for x in block:
            for layer in range(layers):
                term = capacity[layer, pl.ds(x, 1), :] * head0[layer, x + 1]
                base[layer, x] = term + recharge[x] if layer == 0 else term

    over(0, rows, 2, begin)

    for copy in edge_copies:
        copy.wait_recv()
    for side, row, outside in ((0, 0, 0), (1, rows + 1, tile_count - 1)):
        inside = jnp.where(me == outside, 0.0, 1.0)
        for layer in range(layers):
            kc[layer, row:row + 1, :] = edge_got[side, layer:layer + 1, :] * inside
            ka[layer, row:row + 1, :] = edge_got[side, layers + layer:layers + layer + 1, :]

    lane = lax.broadcasted_iota(jnp.int32, (members, width), 1)

    def harmonic(first, second):
        return first * second / (first + second)

    def conduct(head, x):
        return tuple(
            kc[layer, pl.ds(x, 1), :]
            * jnp.exp(ka[layer, pl.ds(x, 1), :] * jnp.minimum(head[layer, x], 0.0))
            for layer in range(layers))

    def link_start(head):
        low = conduct(head, 0)
        here = conduct(head, 1)
        before = tuple(harmonic(a, b) for a, b in zip(low, here))
        for layer in range(layers):
            face_x[layer, 0] = before[layer]
        return here, before

    def link(head, start, stop, carry):
        size = 2

        def step(count, carry):
            here, before = carry
            for offset in range(size):
                x = start + count * size + offset
                after = conduct(head, x + 1)
                ahead = tuple(harmonic(a, b) for a, b in zip(here, after))
                down = None
                for layer in range(layers):
                    face_x[layer, x] = ahead[layer]
                    along = harmonic(here[layer], pltpu.roll(here[layer], width - 1, 1))
                    along = jnp.where(lane == width - 1, 0.0, along)
                    face_y[layer, x - 1] = along
                    diagonal = capacity[layer, pl.ds(x - 1, 1), :] + ahead[layer] + before[layer]
                    diagonal = diagonal + along + pltpu.roll(along, 1, 1)
                    if layer > 0:
                        diagonal = diagonal + down
                    if layer < layers - 1:
                        down = 0.5 * harmonic(here[layer], here[layer + 1])
                        face_z[layer, x - 1] = down
                        diagonal = diagonal + down
                    if layer == 0:
                        diagonal = diagonal + col_cond[pl.ds(x - 1, 1), :]
                    inverse[layer, x - 1] = 1.0 / diagonal
                here, before = after, ahead
            return here, before

        return lax.fori_loop(0, (stop - start) // size, step, carry)

    def relax(head, x, which, with_river):
        now = {layer: head[layer, x] for layer in range(layers)
               if any(abs(layer - other) < 2 for other in which)}
        results = []
        for layer in which:
            along = face_y[layer, x - 1]
            total = source[x - 1] if layer == 0 and with_river else base[layer, x - 1]
            total = total + face_x[layer, x] * head[layer, x + 1]
            total = total + face_x[layer, x - 1] * head[layer, x - 1]
            total = total + along * pltpu.roll(now[layer], width - 1, 1)
            total = total + pltpu.roll(along * now[layer], 1, 1)
            if layer < layers - 1:
                total = total + face_z[layer, x - 1] * now[layer + 1]
            if layer > 0:
                total = total + face_z[layer - 1, x - 1] * now[layer - 1]
            results.append(total * inverse[layer, x - 1])
        return results

    every = list(range(layers))
    lower = every[1:]

    def sweep(index, which, with_river=True):
        def body(block):
            results = [relax(heads[index], x, which, with_river) for x in block]
            for x, result in zip(block, results):
                for layer, value in zip(which, result):
                    heads[index + 1][layer, x] = value
        return body

    def sweep_and_send(index):
        body = sweep(index, every)
        body([1])
        body([rows])
        copies = halo(index + 1)
        over(2, rows, 3, body)
        return copies

    def received(copies):
        for copy in copies:
            copy.wait_recv()

    def by_group(values):
        return jnp.concatenate([values[:, g * LANES:(g + 1) * LANES] for g in range(groups)], axis=0)

    def with_rate(rates, values):
        return jnp.concatenate(
            [rates[g:g + 1, :] * values[:, g * LANES:(g + 1) * LANES] for g in range(groups)], axis=1)

    def fetch(bucket, sections):
        left = jnp.concatenate(halves(by_group(sections)), axis=1)
        wide = slot_range(bucket)
        picked = jnp.dot(left, one_r[:, wide], preferred_element_type=F32)
        value = jnp.zeros((members, slots), F32)
        high = reach_high[own(bucket), :]
        for g in range(groups):
            value = value + jnp.where(high == g, picked[g * members:(g + 1) * members], 0.0)
        fetched[bucket] = value
        flow = weight[own(bucket), :] * value
        for part, term in enumerate(halves(jnp.concatenate([flow, flow], axis=0))):
            spread[part * rows * members:(part + 1) * rows * members, wide] = (
                mask_x[:, wide] * jnp.concatenate([term] * (rows // 2), axis=0))

    def river_sum(first, last):
        wide = slice(first * slots, last * slots)
        sums = dot_rows(spread[:, wide], one_y[:width, wide])
        return (sums[:rows * members] + sums[rows * members:]).reshape(rows, members, width)

    def top_terms(head):
        return jnp.concatenate(halves(head[0, 1:rows + 1].reshape(rows * members, width)), axis=1)

    def leak_part(terms, bucket, parts):
        wide = slot_range(bucket)
        picked = jnp.dot(terms, one_y[:, wide], preferred_element_type=F32)
        value = jnp.zeros((members, slots), F32)
        position = column_x[own(bucket), :]
        for x in range(rows):
            value = value + jnp.where(position == x, picked[x * members:(x + 1) * members], 0.0)
        flow = weight[own(bucket), :] * (fetched[bucket] - value)
        high = reach_high[own(bucket), :]
        split = jnp.concatenate([jnp.where(high == g, flow, 0.0) for g in range(groups)], axis=0)
        sums = dot_rows(jnp.concatenate(halves(split), axis=0), one_r[:LANES, wide])
        sums = sums[:groups * members] + sums[groups * members:]
        for g in range(groups):
            parts[bucket, :, g * LANES:(g + 1) * LANES] = sums[g * members:(g + 1) * members]

    def send_part(step, bucket, parts, got):
        return send(parts.at[bucket], got.at[bucket], leak_send.at[step, bucket],
                    leak_recv.at[step, bucket], owner(bucket))

    def near_leak(parts, got):
        values = parts[NEAR]
        for bucket in near:
            values = values + got[bucket]
        return values

    received(halos)
    link(head0, 1, rows + 1, link_start(head0))
    for bucket in [NEAR] + near:
        if bucket != NEAR:
            first_sections[bucket].wait_recv()
        fetch(bucket, section[...] if bucket == NEAR else sect0[bucket])
    first_sections[FAR].wait_recv()
    fetch(FAR, sect0[FAR])
    source[...] = base[0] + river_sum(0, buckets)
    halos = sweep_and_send(0)
    received(halos)
    halos = sweep_and_send(1)
    received(halos)

    over(1, rows + 1, 4, sweep(2, every[:1]))
    terms = top_terms(head3)
    leak_part(terms, FAR, part1)
    copies = {FAR: send_part(0, FAR, part1, got1)}
    sweep(2, lower)([1])
    sweep(2, lower)([rows])
    halos = halo(3)
    for bucket in near:
        leak_part(terms, bucket, part1)
        copies[bucket] = send_part(0, bucket, part1, got1)
    leak_part(terms, NEAR, part1)
    over(2, rows, 3, sweep(2, lower))
    received(halos)
    half = rows // 2 + 1
    carry = link(head3, 1, half, link_start(head3))

    loads["inflow"].wait()
    rate_copy.wait_recv()
    for bucket in near:
        copies[bucket].wait_recv()
    partial_state[...] = section[...] + with_rate(rate, inflow[...] - near_leak(part1, got1))
    state_copy = send(partial_state, state_got, state_send, state_recv, user(FAR))
    link(head3, half, rows + 1, carry)
    copies[FAR].wait_recv()
    sect1[NEAR] = partial_state[...] - with_rate(rate, got1[FAR])
    second_sections = {
        bucket: send(sect1.at[NEAR], sect1.at[bucket], sect_send.at[1, bucket], sect_recv.at[1, bucket], user(bucket))
        for bucket in near}

    over(1, rows + 1, 4, sweep(3, every, False))
    for bucket in [NEAR] + near:
        if bucket != NEAR:
            second_sections[bucket].wait_recv()
        fetch(bucket, sect1[bucket])
    river[...] = river_sum(0, FAR)
    state_copy.wait_recv()
    fetch(FAR, state_got[...] - with_rate(rate_got, part1[FAR]))
    river[...] = river[...] + river_sum(FAR, buckets)
    source[...] = base[0] + river[...]

    def add_river(block):
        for x in block:
            head4[0, x] = head4[0, x] + river[x - 1] * inverse[0, x - 1]

    add_river([1, rows])
    halos = halo(4)
    over(2, rows, 6, add_river)
    received(halos)
    halos = sweep_and_send(4)
    received(halos)
    over(1, rows + 1, 4, sweep(5, every[:1]))
    terms = top_terms(head6)
    leak_part(terms, FAR, part2)
    copies = {FAR: send_part(1, FAR, part2, got2)}
    for bucket in near:
        leak_part(terms, bucket, part2)
        copies[bucket] = send_part(1, bucket, part2, got2)
    leak_part(terms, NEAR, part2)
    over(1, rows + 1, 4, sweep(5, lower))
    stores = [pltpu.make_async_copy(head6.at[:, 1:rows + 1, m, :], head_out.at[m], store_sem.at[m])
              for m in range(members)]
    for copy in stores:
        copy.start()
    for bucket in near:
        copies[bucket].wait_recv()
    values = near_leak(part2, got2)
    copies[FAR].wait_recv()
    section_out[...] = section[...] + with_rate(rate, inflow[...] - (values + got2[FAR]))
    for copy in stores:
        copy.wait()
    for copy in sends:
        copy.wait_send()


def body(tile_count, head_start, recharge, section_start, inflow, soil_class, class_conduct, class_alpha,
         capacity, river_cell, river_reach, river_cond, reach_rate):
    members, layers, rows, width = head_start.shape
    buckets, slots = river_cell.shape[1:]
    lines = buckets * slots // LANES
    reaches = section_start.shape[1]
    groups = reaches // LANES
    any_spec = pl.BlockSpec(memory_space=pl.ANY)
    smem_spec = pl.BlockSpec(memory_space=pltpu.SMEM)
    vmem_spec = pl.BlockSpec(memory_space=pltpu.VMEM)
    vmem = pltpu.VMEM
    dma = pltpu.SemaphoreType.DMA
    grid = (layers, rows, members, width)
    state = (members, reaches)
    every = buckets * slots
    scratch = [vmem((layers, rows + 2, members, width), F32)] * (PICARD * SWEEPS + 1) + [
        vmem((rows, members, width), F32),
        vmem(state, F32), vmem(state, F32), vmem((layers, rows, width), jnp.int32), vmem((layers, rows, width), F32),
        vmem((lines, LANES), jnp.int32), vmem((lines, LANES), jnp.int32), vmem((lines, LANES), F32),
        vmem((groups, LANES), F32),
        vmem((layers, rows + 8, width), F32), vmem((layers, rows + 8, width), F32),
        vmem(grid, F32), vmem((rows, members, width), F32),
        vmem((layers, rows + 1, members, width), F32), vmem(grid, F32),
        vmem((layers - 1, rows, members, width), F32), vmem(grid, F32), vmem((rows, width), F32),
        vmem((2 * width, every), BF16), vmem((rows * members, every), BF16), vmem((2 * LANES, every), BF16),
        vmem((2 * rows * members, every), BF16),
    ] + [vmem((buckets, slots), F32)] * 5 + [
        vmem((buckets, members, slots), F32), vmem((rows, members, width), F32),
        vmem((2, 2 * layers, width), F32), vmem((2, 2 * layers, width), F32),
    ] + [vmem((buckets,) + state, F32)] * 6 + [vmem(state, F32)] * 2 + [vmem((groups, LANES), F32)] + [
        dma((8,)), dma((members,)), dma((members,)), dma((members,)),
        dma((PICARD * SWEEPS, 2)), dma((PICARD * SWEEPS, 2)), dma((2,)), dma((2,)),
        dma((2, buckets)), dma((2, buckets)), dma((2, buckets)), dma((2, buckets)),
        dma, dma, dma, dma,
    ]
    return pl.pallas_call(
        functools.partial(kernel, tile_count),
        out_shape=(vmem(head_start.shape, F32), vmem(state, F32)),
        in_specs=[any_spec] * 5 + [smem_spec] * 2 + [any_spec] * 5,
        out_specs=(vmem_spec, vmem_spec),
        scratch_shapes=scratch,
        compiler_params=pltpu.CompilerParams(
            collective_id=0, has_side_effects=True, vmem_limit_bytes=52 * 1024 * 1024),
        name="aquifer",
    )(head_start, recharge, section_start, inflow, soil_class, class_conduct, class_alpha, capacity,
      river_cell.reshape(lines, LANES), river_reach.reshape(lines, LANES), river_cond.reshape(lines, LANES),
      reach_rate.reshape(groups, LANES))


def solution(mesh):
    return jax.shard_map(
        functools.partial(body, mesh.shape["space"]),
        mesh=mesh,
        in_specs=(
            P("member", None, "space", None),
            P("member", "space", None),
            P("member", "space"),
            P("member", "space"),
            P(None, "space", None),
            P(),
            P(),
            P(None, "space", None),
            P("space", None, None),
            P("space", None, None),
            P("space", None, None),
            P("space"),
        ),
        out_specs=(P("member", None, "space", None), P("member", "space")),
        check_vma=False,
    )
```

time: 74.7 us -> 72.3 us (0.968)
  Pallas kernels: 68.9 us -> 62.5 us
  local copies, waits for them, and re-layouts: 4.87 us -> 8.65 us
    pallas_call x1, Pallas kernels: 68.9 us -> 62.5 us  [body(): pl.pallas_call(functools.partial(kernel, tile_count), out_shape=(vmem(hea...]
    unnamed x10 -> x24, local copies, waits for them, and re-layouts: 4.87 us -> 8.65 us
where the time goes in v2:
time: 72.3 us; the launch traced here: 71.8 us
  Pallas kernels  62.5 us (86%)
  local copies, waits for them, and re-layouts  8.65 us (12%)
    pallas_call x1, Pallas kernels, body(): pl.pallas_call(functools.partial(kernel, tile_count), out_shape=(vmem(hea...  62.5 us
    unnamed x24, local copies, waits for them, and re-layouts  8.65 us

profile of v2, /device:TPU:1, one launch (start us, length us, event | category | flops | bytes accessed | tf_op | source)
XLA Modules:
  0.0 71.8 jit_solution(7389328461099591100)
XLA Ops:
  0.6 0.0 copy-start.8
  0.6 0.0 copy-start.9
  0.7 0.0 copy-start.10
  0.7 0.7 copy-done.8
  1.3 0.0 copy-done.9
  1.3 0.0 copy-done.10
  1.3 0.0 copy-start
  1.3 0.9 %copy-done = f32[8,32,256]{2,1,0:T(8,128)S(1)} copy-done((f32[8,32,256]{2,1,0:T(8,128)S(1)}, f32[8,32,256]{2,1,0:T(8,128)}, u32[]{:S(2)}) %copy-start) | copy-done | bytes 262168
  2.3 0.0 copy-start.1
  2.3 0.9 %copy-done.1 = s32[4,32,256]{2,1,0:T(8,128)S(1)} copy-done((s32[4,32,256]{2,1,0:T(8,128)S(1)}, s32[4,32,256]{2,1,0:T(8,128)}, u32[]{:S(2)}) %copy-start.1) | copy-done | bytes 131096
  3.2 0.0 copy-start.2
  3.2 0.9 %copy-done.2 = f32[4,32,256]{2,1,0:T(8,128)S(1)} copy-done((f32[4,32,256]{2,1,0:T(8,128)S(1)}, f32[4,32,256]{2,1,0:T(8,128)}, u32[]{:S(2)}) %copy-start.2) | copy-done | bytes 131096
  4.1 0.0 copy-start.3
  4.1 0.8 %copy-done.3 = f32[8,1024]{1,0:T(8,128)S(1)} copy-done((f32[8,1024]{1,0:T(8,128)S(1)}, f32[8,1024]{1,0:T(8,128)}, u32[]{:S(2)}) %copy-start.3) | copy-done | bytes 32792
  4.8 0.0 copy-start.4
  4.8 0.8 %copy-done.4 = f32[8,1024]{1,0:T(8,128)S(1)} copy-done((f32[8,1024]{1,0:T(8,128)S(1)}, f32[8,1024]{1,0:T(8,128)}, u32[]{:S(2)}) %copy-start.4) | copy-done | bytes 32792
  5.6 0.0 copy-start.5
  5.6 0.7 copy-done.5
  6.3 0.0 copy-start.6
  6.3 0.7 copy-done.6
  7.0 0.7 copy-done.7
  7.7 62.5 %aquifer.1 = (f32[8,4,32,256]{3,2,1,0:T(8,128)S(1)}, f32[8,1024]{1,0:T(8,128)S(1)}) custom-call(f32[8,4,32,256]{3,2,1,0:T(8,128)} %head_in.1, f32[8,32,256]{2,1,0:T(8,128)S(1)} %copy-done, f32[8,1024]{1,0:T(8,128)S(1)} %copy-done.3, f32[8,1024]{1,0:T(8,128)S(1)} %copy-done.4, s32[4,32,256]{2,1,0:T(8,128)S(1)} %copy-done.1, f32[12]{0:T(128)S(1)} %copy-done.9, ...), custom_call_target="tpu_custom_call" | custom-call | tf_op jit(solution)/shard_map/aquifer/pallas_call | solution.py:481
  70.2 1.0 %copy.16 = f32[8,4,32,256]{3,2,1,0:T(8,128)} copy(f32[8,4,32,256]{3,2,1,0:T(8,128)S(1)} %get-tuple-element.2) | data formatting | bytes 2097152
  71.2 0.6 copy.17
  (1 shorter events, 0.0 us)
Async XLA Ops:
  0.6 0.7 copy-start.8
  0.6 0.7 copy-start.9
  0.7 0.7 copy-start.10
  1.3 1.0 %copy-start = (f32[8,32,256]{2,1,0:T(8,128)S(1)}, f32[8,32,256]{2,1,0:T(8,128)}, u32[]{:S(2)}) copy-start(f32[8,32,256]{2,1,0:T(8,128)} %recharge_in.1) | copy-start | bytes 786436
  2.3 0.9 %copy-start.1 = (s32[4,32,256]{2,1,0:T(8,128)S(1)}, s32[4,32,256]{2,1,0:T(8,128)}, u32[]{:S(2)}) copy-start(s32[4,32,256]{2,1,0:T(8,128)} %soil_in.1) | copy-start | bytes 393220
  3.2 0.9 %copy-start.2 = (f32[4,32,256]{2,1,0:T(8,128)S(1)}, f32[4,32,256]{2,1,0:T(8,128)}, u32[]{:S(2)}) copy-start(f32[4,32,256]{2,1,0:T(8,128)} %capacity_in.1) | copy-start | bytes 393220
  4.1 0.8 %copy-start.3 = (f32[8,1024]{1,0:T(8,128)S(1)}, f32[8,1024]{1,0:T(8,128)}, u32[]{:S(2)}) copy-start(f32[8,1024]{1,0:T(8,128)} %section_in.1) | copy-start | bytes 98308
  4.8 0.8 %copy-start.4 = (f32[8,1024]{1,0:T(8,128)S(1)}, f32[8,1024]{1,0:T(8,128)}, u32[]{:S(2)}) copy-start(f32[8,1024]{1,0:T(8,128)} %inflow_in.1) | copy-start | bytes 98308
  5.6 0.7 copy-start.5
  6.3 0.7 copy-start.6
  7.0 0.7 copy-start.7

commit v3 on v2

--- a/solution.py
+++ b/solution.py
@@ -450,7 +450,7 @@
     lines = buckets * slots // LANES
     reaches = section_start.shape[1]
     groups = reaches // LANES
-    any_spec = pl.BlockSpec(memory_space=pl.ANY)
+    any_spec = pl.BlockSpec(memory_space=pltpu.HBM)
     smem_spec = pl.BlockSpec(memory_space=pltpu.SMEM)
     vmem_spec = pl.BlockSpec(memory_space=pltpu.VMEM)
     vmem = pltpu.VMEM
@@ -485,7 +485,7 @@
         out_specs=(vmem_spec, vmem_spec),
         scratch_shapes=scratch,
         compiler_params=pltpu.CompilerParams(
-            collective_id=0, has_side_effects=True, vmem_limit_bytes=52 * 1024 * 1024),
+            collective_id=0, has_side_effects=True, vmem_limit_bytes=62 * 1024 * 1024),
         name="aquifer",
     )(head_start, recharge, section_start, inflow, soil_class, class_conduct, class_alpha, capacity,
       river_cell.reshape(lines, LANES), river_reach.reshape(lines, LANES), river_cond.reshape(lines, LANES),

time: 72.3 us -> 64.2 us (0.89)
  local copies, waits for them, and re-layouts: 8.65 us -> 1.59 us
    unnamed x24 -> x2, local copies, waits for them, and re-layouts: 8.65 us -> 1.59 us
where the time goes in v3:
time: 64.2 us; the launch traced here: 64.1 us
  Pallas kernels  61.9 us (96%)
  local copies, waits for them, and re-layouts  1.59 us (2%)
    pallas_call x1, Pallas kernels, body(): pl.pallas_call(functools.partial(kernel, tile_count), out_shape=(vmem(hea...  61.9 us
    unnamed x2, local copies, waits for them, and re-layouts  1.59 us

profile of v3, /device:TPU:1, one launch (start us, length us, event | category | flops | bytes accessed | tf_op | source)
XLA Modules:
  0.0 64.1 jit_solution(2009315888216620981)
XLA Ops:
  0.6 61.9 %aquifer.1 = (f32[8,4,32,256]{3,2,1,0:T(8,128)S(1)}, f32[8,1024]{1,0:T(8,128)S(1)}) custom-call(f32[8,4,32,256]{3,2,1,0:T(8,128)} %head_in.1, f32[8,32,256]{2,1,0:T(8,128)} %recharge_in.1, f32[8,1024]{1,0:T(8,128)} %section_in.1, f32[8,1024]{1,0:T(8,128)} %inflow_in.1, s32[4,32,256]{2,1,0:T(8,128)} %soil_in.1, f32[12]{0:T(128)} %class_conduct.1, ...), custom_call_target="tpu_custom_call" | custom-call | tf_op jit(solution)/shard_map/aquifer/pallas_call | solution.py:481
  62.5 1.0 %copy.16 = f32[8,4,32,256]{3,2,1,0:T(8,128)} copy(f32[8,4,32,256]{3,2,1,0:T(8,128)S(1)} %get-tuple-element.2) | data formatting | bytes 2097152
  63.5 0.6 copy.17

commit v4 on v3

--- a/solution.py
+++ b/solution.py
@@ -31,17 +31,21 @@
     capacity_in, cell_in, reach_in, cond_in, rate_in,
     head_out, section_out,
     head0, head1, head2, head3, head4, head5, head6,
-    recharge, section, inflow, soil, capacity, cell, reach, cond, rate,
-    kc, ka, base, source, face_x, face_y, face_z, inverse, col_cond,
-    one_y, mask_x, one_r, spread, weight, column_x, column_y, reach_high, reach_low, fetched, river,
-    edge, edge_got, sect0, sect1, part1, part2, got1, got2, partial_state, state_got, rate_got,
+    recharge, section, inflow, soil, capacity_own, cell, reach, cond, rate,
+    kc, ka, capacity, base, source, face_x, face_y, face_z, inverse, col_cond, river0, river1,
+    one_y, mask_x, one_r, spread, weight, column_x, column_y, reach_high, reach_low, fetched,
+    edge, edge_got, col_edge, col_got,
+    sect0, sect1, part1, part2, got1, got2, partial_state, state_got, rate_got,
     load_sem, head_sem, recharge_sem, store_sem, halo_send, halo_recv, edge_send, edge_recv,
+    rain_send, rain_recv, col_send, col_recv, river_send, river_recv,
     sect_send, sect_recv, leak_send, leak_recv, state_send, state_recv, rate_send, rate_recv,
 ):
     me = lax.axis_index("space")
     heads = (head0, head1, head2, head3, head4, head5, head6)
     layers, padded, members, width = head0.shape
-    rows = padded - 2
+    deep = SWEEPS
+    rows = padded - 2 * deep
+    first, last = deep, deep + rows - 1
     buckets, slots = weight.shape
     pieces = slots // LANES
     groups = section.shape[1] // LANES
@@ -80,20 +84,20 @@
         lax.fori_loop(0, (stop - start) // size, step, 0)
 
     loads = {}
-    pairs = [("soil", soil_in, soil), ("section", section_in, section), ("rate", rate_in, rate),
+    pairs = [("soil", soil_in, soil), ("capacity", capacity_in, capacity_own), ("section", section_in, section), ("rate", rate_in, rate),
              ("cell", cell_in, cell), ("reach", reach_in, reach), ("cond", cond_in, cond)]
     for index, (name, source_ref, target_ref) in enumerate(pairs):
         loads[name] = pltpu.make_async_copy(source_ref, target_ref, load_sem.at[index])
         loads[name].start()
-    head_loads = [pltpu.make_async_copy(head_in.at[m], head0.at[:, 1:rows + 1, m, :], head_sem.at[m])
+    head_loads = [pltpu.make_async_copy(head_in.at[m], head0.at[:, first:last + 1, m, :], head_sem.at[m])
                   for m in range(members)]
     for copy in head_loads:
         copy.start()
     for index, (name, source_ref, target_ref) in enumerate(
-            [("capacity", capacity_in, capacity), ("inflow", inflow_in, inflow)]):
+            [("inflow", inflow_in, inflow)]):
         loads[name] = pltpu.make_async_copy(source_ref, target_ref, load_sem.at[len(pairs) + index])
         loads[name].start()
-    recharge_loads = [pltpu.make_async_copy(recharge_in.at[m], recharge.at[:, m, :], recharge_sem.at[m])
+    recharge_loads = [pltpu.make_async_copy(recharge_in.at[m], recharge.at[first:last + 1, m, :], recharge_sem.at[m])
                       for m in range(members)]
     for copy in recharge_loads:
         copy.start()
@@ -111,12 +115,57 @@
         match = classes == index
         conduct_of = jnp.where(match, 2.0 * class_conduct[index], conduct_of)
         alpha_of = jnp.where(match, class_alpha[index], alpha_of)
-    kc[:, 1:rows + 1, :] = conduct_of
-    ka[:, 1:rows + 1, :] = alpha_of
-    for side, row in ((0, 0), (1, rows - 1)):
-        for layer in range(layers):
-            edge[side, layer:layer + 1, :] = conduct_of[layer, row:row + 1, :]
-            edge[side, layers + layer:layers + layer + 1, :] = alpha_of[layer, row:row + 1, :]
+    kc[:, first:last + 1, :] = conduct_of
+    ka[:, first:last + 1, :] = alpha_of
+    loads["capacity"].wait()
+    capacity_of = capacity_own[...]
+    capacity[:, first:last + 1, :] = capacity_of
+    packed = [(kc, conduct_of, deep), (ka, alpha_of, deep), (capacity, capacity_of, deep - 1)]
+    for side in range(2):
+        line = 0
+        for _, values, depth in packed:
+            for layer in range(layers):
+                start = 0 if side == 0 else rows - depth
+                edge[side, line:line + depth, :] = values[layer, start:start + depth, :]
+                line += depth
+
+    pl.semaphore_wait(barrier, len(remote))
+
+    loads["section"].wait()
+    loads["rate"].wait()
+    first_sections = {}
+    for bucket in [FAR] + near:
+        first_sections[bucket] = send(
+            section, sect0.at[bucket], sect_send.at[0, bucket], sect_recv.at[0, bucket], user(bucket))
+    rate_copy = send(rate, rate_got, rate_send, rate_recv, user(FAR))
+    beside = [
+        send(edge.at[side], edge_got.at[1 - side], edge_send.at[side], edge_recv.at[1 - side], tile(shift))
+        for side, shift in ((0, -1), (1, 1))]
+
+    def halo(index):
+        step = index // SWEEPS
+        return [
+            send(heads[index].at[:, first:first + deep], heads[index].at[:, last + 1:last + 1 + deep],
+                 halo_send.at[step, 0], halo_recv.at[step, 1], tile(-1)),
+            send(heads[index].at[:, last + 1 - deep:last + 1], heads[index].at[:, 0:deep],
+                 halo_send.at[step, 1], halo_recv.at[step, 0], tile(1)),
+        ]
+
+    def top_halo(values, send_sem, recv_sem):
+        depth = deep - 1
+        return [
+            send(values.at[first:first + depth], values.at[last + 1:last + 1 + depth],
+                 send_sem.at[0], recv_sem.at[1], tile(-1)),
+            send(values.at[last + 1 - depth:last + 1], values.at[first - depth:first],
+                 send_sem.at[1], recv_sem.at[0], tile(1)),
+        ]
+
+    for copy in head_loads:
+        copy.wait()
+    beside += halo(0)
+    for copy in recharge_loads:
+        copy.wait()
+    beside += top_halo(recharge, rain_send, rain_recv)
 
     loads["cell"].wait()
     loads["reach"].wait()
@@ -143,72 +192,44 @@
     y_ids = ids.astype(F32).astype(BF16)
     x_ids = (ids // members).astype(F32).astype(BF16)
     r_ids = (ids % LANES).astype(F32).astype(BF16)
-
-    def build(bucket):
+    flat = lax.broadcasted_iota(jnp.int32, (rows, slots), 0).astype(F32)
+    total = jnp.zeros((2 * rows, width), F32)
+    for bucket in range(buckets):
         wide = slot_range(bucket)
         values = one_hot(y_ids, column_y[own(bucket), :])
         one_y[:width, wide] = values
         one_y[width:, wide] = values
+        terms = jnp.where(flat == column_x[own(bucket), :], weight[own(bucket), :], 0.0)
+        total = total + dot_rows(jnp.concatenate(halves(terms), axis=0), one_y[:width, wide])
+    total = total[:rows] + total[rows:]
+    col_cond[first:last + 1, :] = total
+    col_edge[...] = jnp.zeros(col_edge.shape, F32)
+    col_edge[0, 0:deep - 1, :] = total[0:deep - 1]
+    col_edge[1, 0:deep - 1, :] = total[rows - deep + 1:rows]
+    beside += [
+        send(col_edge.at[side], col_got.at[1 - side], col_send.at[side], col_recv.at[1 - side], tile(shift))
+        for side, shift in ((0, -1), (1, 1))]
+    for bucket in range(buckets):
+        wide = slot_range(bucket)
         mask_x[:, wide] = one_hot(x_ids, column_x[own(bucket), :])
         one_r[:, wide] = one_hot(r_ids, reach_low[own(bucket), :])
 
-    build(0)
-    build(1)
-    build(2)
-
-    pl.semaphore_wait(barrier, len(remote))
-
-    loads["section"].wait()
-    loads["rate"].wait()
-    first_sections = {}
-    for bucket in [FAR] + near:
-        first_sections[bucket] = send(
-            section, sect0.at[bucket], sect_send.at[0, bucket], sect_recv.at[0, bucket], user(bucket))
-    rate_copy = send(rate, rate_got, rate_send, rate_recv, user(FAR))
-    edge_copies = [
-        send(edge.at[side], edge_got.at[1 - side], edge_send.at[side], edge_recv.at[1 - side], tile(shift))
-        for side, shift in ((0, -1), (1, 1))]
-
-    def halo(index):
-        return [
-            send(heads[index].at[:, 1], heads[index].at[:, rows + 1],
-                 halo_send.at[index, 0], halo_recv.at[index, 1], tile(-1)),
-            send(heads[index].at[:, rows], heads[index].at[:, 0],
-                 halo_send.at[index, 1], halo_recv.at[index, 0], tile(1)),
-        ]
-
-    for copy in head_loads:
-        copy.wait()
-    halos = halo(0)
-
-    for bucket in range(3, buckets):
-        build(bucket)
-    flat = lax.broadcasted_iota(jnp.int32, (rows, slots), 0).astype(F32)
-    total = jnp.zeros((2 * rows, width), F32)
-    for bucket in range(buckets):
-        terms = jnp.where(flat == column_x[own(bucket), :], weight[own(bucket), :], 0.0)
-        total = total + dot_rows(jnp.concatenate(halves(terms), axis=0), one_y[:width, slot_range(bucket)])
-    col_cond[...] = total[:rows] + total[rows:]
-
-    loads["capacity"].wait()
-    for copy in recharge_loads:
-        copy.wait()
+    def unpack():
+        for side in range(2):
+            line = 0
+            for target_ref, _, depth in packed:
+                for layer in range(layers):
+                    start = first - depth if side == 0 else last + 1
+                    target_ref[layer, start:start + depth, :] = edge_got[side, line:line + depth, :]
+                    line += depth
+            start = first - deep + 1 if side == 0 else last + 1
+            col_cond[start:start + deep - 1, :] = col_got[side, 0:deep - 1, :]
 
     def begin(block):
         for x in block:
             for layer in range(layers):
-                term = capacity[layer, pl.ds(x, 1), :] * head0[layer, x + 1]
+                term = capacity[layer, pl.ds(x, 1), :] * head0[layer, x]
                 base[layer, x] = term + recharge[x] if layer == 0 else term
-
-    over(0, rows, 2, begin)
-
-    for copy in edge_copies:
-        copy.wait_recv()
-    for side, row, outside in ((0, 0, 0), (1, rows + 1, tile_count - 1)):
-        inside = jnp.where(me == outside, 0.0, 1.0)
-        for layer in range(layers):
-            kc[layer, row:row + 1, :] = edge_got[side, layer:layer + 1, :] * inside
-            ka[layer, row:row + 1, :] = edge_got[side, layers + layer:layers + layer + 1, :]
 
     lane = lax.broadcasted_iota(jnp.int32, (members, width), 1)
 
@@ -222,9 +243,9 @@
             for layer in range(layers))
 
     def link_start(head):
-        low = conduct(head, 0)
+        before_rows = conduct(head, 0)
         here = conduct(head, 1)
-        before = tuple(harmonic(a, b) for a, b in zip(low, here))
+        before = tuple(harmonic(a, b) for a, b in zip(before_rows, here))
         for layer in range(layers):
             face_x[layer, 0] = before[layer]
         return here, before
@@ -237,24 +258,26 @@
             for offset in range(size):
                 x = start + count * size + offset
                 after = conduct(head, x + 1)
-                ahead = tuple(harmonic(a, b) for a, b in zip(here, after))
+                shut = ((x == first - 1) & (me == 0)) | ((x == last) & (me == tile_count - 1))
+                inside = jnp.where(shut, 0.0, 1.0)
+                ahead = tuple(inside * harmonic(a, b) for a, b in zip(here, after))
                 down = None
                 for layer in range(layers):
                     face_x[layer, x] = ahead[layer]
                     along = harmonic(here[layer], pltpu.roll(here[layer], width - 1, 1))
                     along = jnp.where(lane == width - 1, 0.0, along)
-                    face_y[layer, x - 1] = along
-                    diagonal = capacity[layer, pl.ds(x - 1, 1), :] + ahead[layer] + before[layer]
+                    face_y[layer, x] = along
+                    diagonal = capacity[layer, pl.ds(x, 1), :] + ahead[layer] + before[layer]
                     diagonal = diagonal + along + pltpu.roll(along, 1, 1)
                     if layer > 0:
                         diagonal = diagonal + down
                     if layer < layers - 1:
                         down = 0.5 * harmonic(here[layer], here[layer + 1])
-                        face_z[layer, x - 1] = down
+                        face_z[layer, x] = down
                         diagonal = diagonal + down
                     if layer == 0:
-                        diagonal = diagonal + col_cond[pl.ds(x - 1, 1), :]
-                    inverse[layer, x - 1] = 1.0 / diagonal
+                        diagonal = diagonal + col_cond[pl.ds(x, 1), :]
+                    inverse[layer, x] = 1.0 / diagonal
                 here, before = after, ahead
             return here, before
 
@@ -265,17 +288,17 @@
                if any(abs(layer - other) < 2 for other in which)}
         results = []
         for layer in which:
-            along = face_y[layer, x - 1]
-            total = source[x - 1] if layer == 0 and with_river else base[layer, x - 1]
+            along = face_y[layer, x]
+            total = source[x] if layer == 0 and with_river else base[layer, x]
             total = total + face_x[layer, x] * head[layer, x + 1]
             total = total + face_x[layer, x - 1] * head[layer, x - 1]
             total = total + along * pltpu.roll(now[layer], width - 1, 1)
             total = total + pltpu.roll(along * now[layer], 1, 1)
             if layer < layers - 1:
-                total = total + face_z[layer, x - 1] * now[layer + 1]
+                total = total + face_z[layer, x] * now[layer + 1]
             if layer > 0:
-                total = total + face_z[layer - 1, x - 1] * now[layer - 1]
-            results.append(total * inverse[layer, x - 1])
+                total = total + face_z[layer - 1, x] * now[layer - 1]
+            results.append(total * inverse[layer, x])
         return results
 
     every = list(range(layers))
@@ -288,14 +311,6 @@
                 for layer, value in zip(which, result):
                     heads[index + 1][layer, x] = value
         return body
-
-    def sweep_and_send(index):
-        body = sweep(index, every)
-        body([1])
-        body([rows])
-        copies = halo(index + 1)
-        over(2, rows, 3, body)
-        return copies
 
     def received(copies):
         for copy in copies:
@@ -322,13 +337,13 @@
             spread[part * rows * members:(part + 1) * rows * members, wide] = (
                 mask_x[:, wide] * jnp.concatenate([term] * (rows // 2), axis=0))
 
-    def river_sum(first, last):
-        wide = slice(first * slots, last * slots)
+    def river_sum(start, stop):
+        wide = slice(start * slots, stop * slots)
         sums = dot_rows(spread[:, wide], one_y[:width, wide])
         return (sums[:rows * members] + sums[rows * members:]).reshape(rows, members, width)
 
     def top_terms(head):
-        return jnp.concatenate(halves(head[0, 1:rows + 1].reshape(rows * members, width)), axis=1)
+        return jnp.concatenate(halves(head[0, first:last + 1].reshape(rows * members, width)), axis=1)
 
     def leak_part(terms, bucket, parts):
         wide = slot_range(bucket)
@@ -355,34 +370,43 @@
             values = values + got[bucket]
         return values
 
-    received(halos)
-    link(head0, 1, rows + 1, link_start(head0))
     for bucket in [NEAR] + near:
         if bucket != NEAR:
             first_sections[bucket].wait_recv()
         fetch(bucket, section[...] if bucket == NEAR else sect0[bucket])
+    received(beside)
+    unpack()
+    over(1, padded - 1, 2, begin)
+    half = padded // 2
+    carry = link(head0, 1, half, link_start(head0))
     first_sections[FAR].wait_recv()
     fetch(FAR, sect0[FAR])
-    source[...] = base[0] + river_sum(0, buckets)
-    halos = sweep_and_send(0)
-    received(halos)
-    halos = sweep_and_send(1)
-    received(halos)
-
-    over(1, rows + 1, 4, sweep(2, every[:1]))
+    river0[first:last + 1] = river_sum(0, buckets)
+    river_copies = top_halo(river0, river_send.at[0], river_recv.at[0])
+    link(head0, half, padded - 1, carry)
+    outer = [first - 2, first - 1, last + 1, last + 2]
+    source[first:last + 1] = base[0, first:last + 1] + river0[first:last + 1]
+    over(first, last + 1, 4, sweep(0, every))
+    received(river_copies)
+    for x in outer:
+        source[x] = base[0, x] + river0[x]
+    sweep(0, every)(outer[:2])
+    sweep(0, every)(outer[2:])
+    over(first - 1, last + 2, 2, sweep(1, every))
+
+    over(first, last + 1, 4, sweep(2, every[:1]))
     terms = top_terms(head3)
     leak_part(terms, FAR, part1)
     copies = {FAR: send_part(0, FAR, part1, got1)}
-    sweep(2, lower)([1])
-    sweep(2, lower)([rows])
-    halos = halo(3)
+    sweep(2, lower)(list(range(first, first + deep)))
+    sweep(2, lower)(list(range(last + 1 - deep, last + 1)))
+    halos = halo(SWEEPS)
     for bucket in near:
         leak_part(terms, bucket, part1)
         copies[bucket] = send_part(0, bucket, part1, got1)
     leak_part(terms, NEAR, part1)
-    over(2, rows, 3, sweep(2, lower))
+    over(first + deep, last + 1 - deep, 2, sweep(2, lower))
     received(halos)
-    half = rows // 2 + 1
     carry = link(head3, 1, half, link_start(head3))
 
     loads["inflow"].wait()
@@ -391,35 +415,37 @@
         copies[bucket].wait_recv()
     partial_state[...] = section[...] + with_rate(rate, inflow[...] - near_leak(part1, got1))
     state_copy = send(partial_state, state_got, state_send, state_recv, user(FAR))
-    link(head3, half, rows + 1, carry)
+    link(head3, half, padded - 1, carry)
     copies[FAR].wait_recv()
     sect1[NEAR] = partial_state[...] - with_rate(rate, got1[FAR])
     second_sections = {
         bucket: send(sect1.at[NEAR], sect1.at[bucket], sect_send.at[1, bucket], sect_recv.at[1, bucket], user(bucket))
         for bucket in near}
 
-    over(1, rows + 1, 4, sweep(3, every, False))
+    over(1, padded - 1, 4, sweep(3, every, False))
     for bucket in [NEAR] + near:
         if bucket != NEAR:
             second_sections[bucket].wait_recv()
         fetch(bucket, sect1[bucket])
-    river[...] = river_sum(0, FAR)
+    river1[first:last + 1] = river_sum(0, FAR)
     state_copy.wait_recv()
     fetch(FAR, state_got[...] - with_rate(rate_got, part1[FAR]))
-    river[...] = river[...] + river_sum(FAR, buckets)
-    source[...] = base[0] + river[...]
+    river1[first:last + 1] = river1[first:last + 1] + river_sum(FAR, buckets)
+    river_copies = top_halo(river1, river_send.at[1], river_recv.at[1])
 
     def add_river(block):
         for x in block:
-            head4[0, x] = head4[0, x] + river[x - 1] * inverse[0, x - 1]
-
-    add_river([1, rows])
-    halos = halo(4)
-    over(2, rows, 6, add_river)
-    received(halos)
-    halos = sweep_and_send(4)
-    received(halos)
-    over(1, rows + 1, 4, sweep(5, every[:1]))
+            source[x] = base[0, x] + river1[x]
+            head4[0, x] = head4[0, x] + river1[x] * inverse[0, x]
+
+    over(first, last + 1, 4, add_river)
+    over(first + 1, last, 3, sweep(4, every))
+    over(first + 2, last - 1, 4, sweep(5, every))
+    received(river_copies)
+    add_river(outer)
+    sweep(4, every)([first - 1, first])
+    sweep(4, every)([last, last + 1])
+    sweep(5, every[:1])([first, first + 1, last - 1, last])
     terms = top_terms(head6)
     leak_part(terms, FAR, part2)
     copies = {FAR: send_part(1, FAR, part2, got2)}
@@ -427,8 +453,9 @@
         leak_part(terms, bucket, part2)
         copies[bucket] = send_part(1, bucket, part2, got2)
     leak_part(terms, NEAR, part2)
-    over(1, rows + 1, 4, sweep(5, lower))
-    stores = [pltpu.make_async_copy(head6.at[:, 1:rows + 1, m, :], head_out.at[m], store_sem.at[m])
+    sweep(5, lower)([first, first + 1])
+    sweep(5, lower)([last - 1, last])
+    stores = [pltpu.make_async_copy(head6.at[:, first:last + 1, m, :], head_out.at[m], store_sem.at[m])
               for m in range(members)]
     for copy in stores:
         copy.start()
@@ -455,26 +482,31 @@
     vmem_spec = pl.BlockSpec(memory_space=pltpu.VMEM)
     vmem = pltpu.VMEM
     dma = pltpu.SemaphoreType.DMA
-    grid = (layers, rows, members, width)
+    padded = rows + 2 * SWEEPS
+    lined = -(-padded // 8) * 8
+    grid = (layers, padded, members, width)
     state = (members, reaches)
     every = buckets * slots
-    scratch = [vmem((layers, rows + 2, members, width), F32)] * (PICARD * SWEEPS + 1) + [
-        vmem((rows, members, width), F32),
+    package = layers * (3 * SWEEPS - 1)
+    scratch = [vmem(grid, F32)] * (PICARD * SWEEPS + 1) + [
+        vmem((padded, members, width), F32),
         vmem(state, F32), vmem(state, F32), vmem((layers, rows, width), jnp.int32), vmem((layers, rows, width), F32),
         vmem((lines, LANES), jnp.int32), vmem((lines, LANES), jnp.int32), vmem((lines, LANES), F32),
         vmem((groups, LANES), F32),
-        vmem((layers, rows + 8, width), F32), vmem((layers, rows + 8, width), F32),
-        vmem(grid, F32), vmem((rows, members, width), F32),
-        vmem((layers, rows + 1, members, width), F32), vmem(grid, F32),
-        vmem((layers - 1, rows, members, width), F32), vmem(grid, F32), vmem((rows, width), F32),
+        vmem((layers, lined, width), F32), vmem((layers, lined, width), F32), vmem((layers, lined, width), F32),
+        vmem(grid, F32), vmem((padded, members, width), F32),
+        vmem(grid, F32), vmem(grid, F32), vmem((layers - 1,) + grid[1:], F32), vmem(grid, F32),
+        vmem((lined, width), F32), vmem((padded, members, width), F32), vmem((padded, members, width), F32),
         vmem((2 * width, every), BF16), vmem((rows * members, every), BF16), vmem((2 * LANES, every), BF16),
         vmem((2 * rows * members, every), BF16),
     ] + [vmem((buckets, slots), F32)] * 5 + [
-        vmem((buckets, members, slots), F32), vmem((rows, members, width), F32),
-        vmem((2, 2 * layers, width), F32), vmem((2, 2 * layers, width), F32),
+        vmem((buckets, members, slots), F32),
+        vmem((2, package, width), F32), vmem((2, package, width), F32),
+        vmem((2, 8, width), F32), vmem((2, 8, width), F32),
     ] + [vmem((buckets,) + state, F32)] * 6 + [vmem(state, F32)] * 2 + [vmem((groups, LANES), F32)] + [
         dma((8,)), dma((members,)), dma((members,)), dma((members,)),
-        dma((PICARD * SWEEPS, 2)), dma((PICARD * SWEEPS, 2)), dma((2,)), dma((2,)),
+        dma((PICARD, 2)), dma((PICARD, 2)), dma((2,)), dma((2,)),
+        dma((2,)), dma((2,)), dma((2,)), dma((2,)), dma((PICARD, 2)), dma((PICARD, 2)),
         dma((2, buckets)), dma((2, buckets)), dma((2, buckets)), dma((2, buckets)),
         dma, dma, dma, dma,
     ]

time: 64.2 us -> 57.6 us (0.90)
  Pallas kernels: 61.9 us -> 55.3 us
    pallas_call x1, Pallas kernels: 61.9 us -> 55.3 us  [body(): pl.pallas_call(functools.partial(kernel, tile_count), out_shape=(vmem(hea...]
where the time goes in v4:
time: 57.6 us; the launch traced here: 57.5 us
  Pallas kernels  55.3 us (96%)
  local copies, waits for them, and re-layouts  1.59 us (3%)
  between operations  0.64 us (1%)
    pallas_call x1, Pallas kernels, body(): pl.pallas_call(functools.partial(kernel, tile_count), out_shape=(vmem(hea...  55.3 us
    unnamed x2, local copies, waits for them, and re-layouts  1.59 us

profile of v4, /device:TPU:1, one launch (start us, length us, event | category | flops | bytes accessed | tf_op | source)
XLA Modules:
  0.0 57.5 jit_solution(8233268460881554308)
XLA Ops:
  0.6 55.3 %aquifer.1 = (f32[8,4,32,256]{3,2,1,0:T(8,128)S(1)}, f32[8,1024]{1,0:T(8,128)S(1)}) custom-call(f32[8,4,32,256]{3,2,1,0:T(8,128)} %head_in.1, f32[8,32,256]{2,1,0:T(8,128)} %recharge_in.1, f32[8,1024]{1,0:T(8,128)} %section_in.1, f32[8,1024]{1,0:T(8,128)} %inflow_in.1, s32[4,32,256]{2,1,0:T(8,128)} %soil_in.1, f32[12]{0:T(128)} %class_conduct.1, ...), custom_call_target="tpu_custom_call" | custom-call | tf_op jit(solution)/shard_map/aquifer/pallas_call | solution.py:513
  55.9 1.0 %copy.16 = f32[8,4,32,256]{3,2,1,0:T(8,128)} copy(f32[8,4,32,256]{3,2,1,0:T(8,128)S(1)} %get-tuple-element.2) | data formatting | bytes 2097152
  56.9 0.6 %copy.17 = f32[8,1024]{1,0:T(8,128)} copy(f32[8,1024]{1,0:T(8,128)S(1)} %get-tuple-element.3) | data formatting | bytes 65536
